TPU v7x, 256 devices: a whole 4x4x8 slice. The times are simulated.
256 devices in a mesh: pb: 64 (over x, y, z_lo), col: 4 (over z_hi, core).
Axes of the slice: x: 4, y: 4, z: 8 (z_hi: 2, z_lo: 4; z = z_hi * 4 + z_lo), core: 2. Of those that a mesh axis runs over, the one named last changes fastest.
Arguments:
- vertex: bfloat16 [3, 256, 448, 896], P(None, 'pb', 'col'), may hold values from -6 to 6
- loop_blocks: bfloat16 [3, 256, 448, 896], P(None, ('pb', 'col')), may hold values from -0.013671875 to 0.013671875
- mixing: float32 [6, 256], replicated, may hold values from -1 to 1
- bond_offsets: int32 [7, 3], replicated, may hold values from -1 to 1
Outputs:
- new_vertex: bfloat16 [3, 256, 448, 896], P(None, 'pb', 'col')
All inputs are finite; a program needn't handle non-finite values.
Results may differ from a plain program's by a relative error of at most 0.007.
Values may be sent and summed in bfloat16 or wider, within the bound.
No kernel may reach another device: no remote copies, remote signals or barrier semaphores. Data moves between devices by JAX's collectives and lax.ppermute only.
A program may use at most 64 MiB of HBM per device.

v0:
```python
import functools
import math

import jax
import jax.numpy as jnp
from jax import lax
from jax.experimental import pallas as pl
from jax.experimental.pallas import tpu as pltpu
from jax.sharding import PartitionSpec as P

NB = 7
MX = 8
LANES = 128
PARTS = 4


step_length = 0.25


def mesh_coords(momenta, mesh_y, mesh_z):
    flat_index = jnp.arange(momenta, dtype=jnp.int32)
    coord_x = flat_index // (mesh_y * mesh_z)
    coord_y = flat_index // mesh_z % mesh_y
    coord_z = flat_index % mesh_z
    return (coord_x, coord_y, coord_z)


def phase_tables(momenta, mesh_x, mesh_y, mesh_z):
    coord_x, coord_y, coord_z = mesh_coords(momenta, mesh_y, mesh_z)
    phase_index = (
        coord_x[:, None] * coord_x[None, :] * (mesh_y * mesh_z)
        + coord_y[:, None] * coord_y[None, :] * (mesh_x * mesh_z)
        + coord_z[:, None] * coord_z[None, :] * (mesh_x * mesh_y)
    ) % momenta
    angles = phase_index.astype(jnp.float32) * (2.0 * math.pi / momenta)
    cosine = jnp.cos(angles)
    sine_part = jnp.sin(angles)
    forward = jnp.stack([jnp.stack([cosine, sine_part], 1), jnp.stack([-sine_part, cosine], 1)]) * (
        1.0 / momenta
    )
    backward = jnp.stack([jnp.stack([cosine, -sine_part], 1), jnp.stack([sine_part, cosine], 1)])
    return (forward.astype(jnp.bfloat16), backward.astype(jnp.bfloat16))


def pieces_of(values, axis):
    high = lax.reduce_precision(values, 8, 7)
    rest = values - high
    middle = lax.reduce_precision(rest, 8, 7)
    return jnp.concatenate([high, middle, rest - middle], axis=axis).astype(jnp.bfloat16)


def shifted_slots(bond_offsets, sign, sides):
    mesh_x, mesh_y, mesh_z = sides
    coords = mesh_coords(mesh_x * mesh_y * mesh_z, mesh_y, mesh_z)
    slot = 0
    for axis, side in enumerate(sides):
        moved = jnp.mod(coords[axis][None, :] + sign * bond_offsets[:, axis][:, None], side)
        slot = slot * side + moved
    return slot


def shifted_weights(mixing, bond_offsets, column_bonds, row_count, sides):
    count, momenta = mixing.shape
    f32 = jnp.float32
    slots = shifted_slots(bond_offsets, 1, sides)
    source = lax.broadcasted_iota(jnp.int32, (momenta, NB, momenta), 0)
    picks = (source == slots[None]).astype(jnp.bfloat16).reshape(momenta, NB * momenta)
    first = jnp.dot(pieces_of(mixing, 0), picks, preferred_element_type=f32)
    first = first[:count] + first[count : 2 * count] + first[2 * count :]
    first = first.reshape(count * NB, momenta)
    row = lax.broadcasted_iota(jnp.int32, (count * NB, count * LANES), 0)
    lane = lax.broadcasted_iota(jnp.int32, (count * NB, count * LANES), 1)
    spot = lane % LANES
    spread = (row == lane // LANES * NB + spot % NB) & (spot < row_count)
    spread = spread.astype(jnp.bfloat16)
    wide = jnp.dot(pieces_of(first.T, 0), spread, preferred_element_type=f32)
    wide = wide[:momenta] + wide[momenta : 2 * momenta] + wide[2 * momenta :]
    slots = shifted_slots(column_bonds, -1, sides)
    target = lax.broadcasted_iota(jnp.int32, (NB, momenta, momenta), 2)
    picks = (target == slots[:, :, None]).astype(jnp.bfloat16)
    length = NB * row_count
    spans = -(-length // LANES)
    return pl.pallas_call(
        functools.partial(weights_kernel, row_count),
        in_specs=[whole(), whole()],
        out_specs=whole(),
        out_shape=jax.ShapeDtypeStruct((count, momenta, spans * LANES), f32),
        scratch_shapes=[pltpu.VMEM((NB, count, momenta, LANES), f32)],
        compiler_params=pltpu.CompilerParams(vmem_limit_bytes=32 * 1024 * 1024),
    )(picks, pieces_of(wide, 1))


def weights_kernel(row_count, picks_ref, wide_ref, out_ref, tmp_ref):
    count, momenta, _ = out_ref.shape
    width = count * LANES
    spans = out_ref.shape[2] // LANES

    def pick(n, carry):
        both = jnp.dot(picks_ref[n], wide_ref[...], preferred_element_type=jnp.float32)
        both = both[:, :width] + both[:, width : 2 * width] + both[:, 2 * width :]
        for j in range(count):
            tmp_ref[n, j] = both[:, j * LANES : (j + 1) * LANES]
        return carry

    lax.fori_loop(0, NB, pick, 0)
    edge = NB * row_count - (spans - 1) * LANES

    def pack(j, carry):
        for i in range(spans):
            tile = packed(lambda s, _: tmp_ref[s, j], i, NB, row_count)
            if i == spans - 1:
                tile = jnp.where(lane_ids(momenta) < edge, tile, 0.0)
            out_ref[j, :, i * LANES : (i + 1) * LANES] = tile
        return carry

    lax.fori_loop(0, count, pack, 0)


def lane_ids(rows):
    return lax.broadcasted_iota(jnp.int32, (rows, LANES), 1)


def moved(tile, shift):
    shift = shift % LANES
    return pltpu.roll(tile, shift, 1) if shift else tile


def cut(get, start, length, last):
    index, offset = divmod(start, LANES)
    tile = moved(get(index), -offset)
    if offset + length <= LANES or index == last:
        return tile
    rest = moved(get(index + 1), LANES - offset)
    return jnp.where(lane_ids(tile.shape[0]) < LANES - offset, tile, rest)


def packed(get, j, segments, length):
    low, high = j * LANES, (j + 1) * LANES
    out = None
    for s in range(segments):
        for i in range(-(-length // LANES)):
            first = s * length + i * LANES
            stop = s * length + min((i + 1) * LANES, length)
            if stop <= low or first >= high:
                continue
            tile = moved(get(s, i), first - low)
            begin = max(first, low) - low
            out = tile if out is None else jnp.where(lane_ids(tile.shape[0]) < begin, out, tile)
    return out


def spread_kernel(v_ref, out_ref, tmp_ref):
    channels, mesh_z, row_count, width = v_ref.shape
    groups, tiles, inner, _ = out_ref.shape
    order = width // 2
    narrow = order // groups

    def turn(t, carry):
        for z in range(mesh_z):
            block = v_ref[t, z].astype(jnp.float32)
            zeros = jnp.zeros((LANES - row_count, width), jnp.float32)
            turned = jnp.concatenate([block, zeros], axis=0).T
            for p in range(2):
                for n in range(narrow):
                    start = p * order + n * groups
                    tmp_ref[t * narrow + n, pl.ds(2 * z + p, groups, stride=inner), :] = turned[
                        start : start + groups
                    ]
        return carry

    lax.fori_loop(0, channels, turn, 0)
    share = groups // PARTS

    def pack(c, carry):
        rows = pl.ds(pl.multiple_of(c * share * inner, share * inner), share * inner)
        for j in range(tiles):
            tile = packed(lambda s, _: tmp_ref[s, rows], j, channels * narrow, row_count)
            out_ref[pl.ds(c * share, share), j] = tile.reshape(share, inner, LANES).astype(
                jnp.bfloat16
            )
        return carry

    lax.fori_loop(0, PARTS, pack, 0)


def whole():
    return pl.BlockSpec(memory_space=pltpu.VMEM)


def spread_rows(vertex, groups):
    channels, mesh_z, row_count, width = vertex.shape
    narrow = width // 2 // groups
    tiles = -(-channels * narrow * row_count // LANES)
    return pl.pallas_call(
        spread_kernel,
        in_specs=[whole()],
        out_specs=whole(),
        out_shape=jax.ShapeDtypeStruct((groups, tiles, 2 * mesh_z, LANES), jnp.bfloat16),
        scratch_shapes=[
            pltpu.VMEM((channels * narrow, groups * 2 * mesh_z, LANES), jnp.float32)
        ],
        compiler_params=pltpu.CompilerParams(vmem_limit_bytes=32 * 1024 * 1024),
    )(vertex)


def transform_kernel(
    length, x_ref, forward_ref, backward_ref, w_hbm, out_ref, lat_ref, mix_ref, w_ref, sem
):
    f32, bf16 = jnp.float32, jnp.bfloat16
    rows = forward_ref.shape[0]
    tiles = x_ref.shape[1]
    spans = -(-length // LANES)
    copy = pltpu.make_async_copy(w_hbm, w_ref, sem)
    copy.start()

    def x_tile(j):
        return x_ref[:, j].astype(f32).reshape(rows, LANES)

    def by_pairs(step):
        def pair(i, carry):
            step([2 * i, 2 * i + 1])
            return carry

        lax.fori_loop(0, tiles // 2, pair, 0)
        if tiles % 2:
            step([tiles - 1])

    def forward(places):
        x = jnp.concatenate([x_tile(j).astype(bf16) for j in places], axis=1)
        lattice = jnp.dot(forward_ref[...], x, preferred_element_type=f32).astype(bf16)
        for place, j in enumerate(places):
            lat_ref[j] = lattice[:, place * LANES : (place + 1) * LANES]

    by_pairs(forward)
    copy.wait()
    share = rows // PARTS

    def mix(c, carry):
        part = pl.ds(pl.multiple_of(c * share, share), share)
        half = pl.ds(pl.multiple_of(c % (PARTS // 2) * share, share), share)
        mixed = {}
        for i in range(spans):
            lanes = slice(i * LANES, (i + 1) * LANES)
            source = [
                cut(
                    lambda j: lat_ref[j, part].astype(f32),
                    t * length + i * LANES,
                    min(LANES, length - i * LANES),
                    tiles - 1,
                )
                for t in range(3)
            ]
            for t in range(3):
                summed = (
                    w_ref[2 * t, half, lanes] * source[(t + 1) % 3]
                    + w_ref[2 * t + 1, half, lanes] * source[(t + 2) % 3]
                )
                mixed[t, i] = summed.astype(bf16)
        for j in range(tiles):
            tile = packed(lambda t, i: mixed[t, i].astype(f32), j, 3, length)
            mix_ref[j, part] = tile.astype(bf16)
        return carry

    lax.fori_loop(0, PARTS, mix, 0)

    def backward(places):
        mixed = jnp.concatenate([mix_ref[j] for j in places], axis=1)
        projected = jnp.dot(backward_ref[...], mixed, preferred_element_type=f32).astype(bf16)
        for place, j in enumerate(places):
            part = projected[:, place * LANES : (place + 1) * LANES].astype(f32)
            out_ref[j] = (x_tile(j) + part).astype(bf16)

    by_pairs(backward)


def transform(x, forward, backward, w, length):
    groups, tiles, inner, _ = x.shape
    rows = groups * inner
    return pl.pallas_call(
        functools.partial(transform_kernel, length),
        in_specs=[whole(), whole(), whole(), pl.BlockSpec(memory_space=pl.ANY)],
        out_specs=whole(),
        out_shape=jax.ShapeDtypeStruct((tiles, rows, LANES), jnp.bfloat16),
        scratch_shapes=[
            pltpu.VMEM((tiles, rows, LANES), jnp.bfloat16),
            pltpu.VMEM((tiles, rows, LANES), jnp.bfloat16),
            pltpu.VMEM(w.shape, jnp.float32),
            pltpu.SemaphoreType.DMA,
        ],
        compiler_params=pltpu.CompilerParams(vmem_limit_bytes=40 * 1024 * 1024),
    )(x, forward, backward, pltpu.with_memory_space_constraint(w, pltpu.HBM))


def products_kernel(t, u_ref, loop_hbm, out_ref, loop_ref, tall_ref, wide_ref, sem):
    f32, bf16 = jnp.float32, jnp.bfloat16
    tiles, _, cols, groups, _ = u_ref.shape
    order = tall_ref.shape[0] // 2
    narrow = order // groups
    depth = cols * LANES
    row_count = out_ref.shape[1]
    copy = pltpu.make_async_copy(loop_hbm.at[t], loop_ref, sem)
    copy.start()

    def place(k, carry):
        here = pl.ds(pl.multiple_of(k * LANES, LANES), LANES)
        there = pl.ds(pl.multiple_of(depth + k * LANES, LANES), LANES)
        for n in range(narrow):
            real, imag = [
                cut(
                    lambda j: u_ref[j, p, k].astype(f32),
                    (t * narrow + n) * row_count,
                    row_count,
                    tiles - 1,
                )
                for p in range(2)
            ]
            minus = (-imag).astype(bf16)
            real, imag = real.astype(bf16), imag.astype(bf16)
            upper = slice(n * groups, (n + 1) * groups)
            lower = slice(order + n * groups, order + (n + 1) * groups)
            tall_ref[upper, here] = real
            tall_ref[lower, here] = imag
            wide_ref[upper, here] = real
            wide_ref[upper, there] = minus
            wide_ref[lower, here] = imag
            wide_ref[lower, there] = real
        return carry

    lax.fori_loop(0, cols, place, 0)
    copy.wait()
    middle = lax.dot_general(
        tall_ref[...], loop_ref[...], (((0,), (0,)), ((), ())), preferred_element_type=f32
    ).astype(bf16)
    change = lax.dot_general(
        middle, wide_ref[...], (((1,), (1,)), ((), ())), preferred_element_type=f32
    )
    increment = (step_length * change).astype(bf16)
    for k in range(cols):
        out_ref[k] = increment[k * LANES : k * LANES + row_count]


def products(t, u, loops, row_count):
    cols = u.shape[2]
    rows, depth = loops.shape[1:]
    return pl.pallas_call(
        functools.partial(products_kernel, t),
        in_specs=[whole(), pl.BlockSpec(memory_space=pl.ANY)],
        out_specs=whole(),
        out_shape=jax.ShapeDtypeStruct((cols, row_count, rows), jnp.bfloat16),
        scratch_shapes=[
            pltpu.VMEM((rows, depth), jnp.bfloat16),
            pltpu.VMEM((rows, depth // 2), jnp.bfloat16),
            pltpu.VMEM((rows, depth), jnp.bfloat16),
            pltpu.SemaphoreType.DMA,
        ],
        compiler_params=pltpu.CompilerParams(vmem_limit_bytes=32 * 1024 * 1024),
    )(u, pltpu.with_memory_space_constraint(loops, pltpu.HBM))


def per_device(vertex, loop_blocks, mixing, bond_offsets):
    groups = lax.axis_size("pb")
    cols = lax.axis_size("col")
    mesh_z = vertex.shape[1]
    row_count = vertex.shape[2]
    order = vertex.shape[3] // 2
    narrow = order // groups
    momenta = mesh_z * groups
    mesh_y = groups // MX
    sent = spread_rows(vertex, groups)
    gathered = lax.all_to_all(sent, "pb", split_axis=0, concat_axis=0, tiled=True)

    forward, backward = phase_tables(momenta, MX, mesh_y, mesh_z)
    forward = forward.transpose(2, 3, 1, 0).reshape(2 * momenta, 2 * momenta)
    backward = backward.transpose(3, 2, 0, 1).reshape(2 * momenta, 2 * momenta)
    bond = jnp.arange(NB, dtype=jnp.int32)
    own = (jnp.arange(narrow, dtype=jnp.int32) * groups + lax.axis_index("pb")) % NB
    column_bonds = jnp.sum(
        jnp.where((own[:, None] == bond[None, :])[:, :, None], bond_offsets[None], 0), axis=1
    )
    w = shifted_weights(mixing, bond_offsets, column_bonds, row_count, (MX, mesh_y, mesh_z))
    lane_pad = LANES - row_count
    loops = loop_blocks.reshape(3, order, 2, cols, row_count)
    loops = jnp.pad(loops, [(0, 0)] * 4 + [(0, lane_pad)]).reshape(3, order, 2, cols * LANES)
    loop_re, loop_im = loops[:, :, 0], loops[:, :, 1]
    loops = jnp.concatenate(
        [
            jnp.concatenate([loop_re, loop_im], axis=2),
            jnp.concatenate([-loop_im, loop_re], axis=2),
        ],
        axis=1,
    )

    united = transform(gathered, forward, backward, w, narrow * row_count)
    tiles = united.shape[0]
    united = united.reshape(tiles, momenta, 2, LANES).transpose(1, 0, 2, 3)
    sent = lax.all_to_all(united, ("pb", "col"), split_axis=0, concat_axis=0, tiled=True)
    u = sent.reshape(groups, cols, tiles, 2, LANES).transpose(2, 3, 1, 0, 4)
    mine = lax.axis_index("col")
    parts = []
    for t in range(3):
        if t:
            u, parts[-1][1] = lax.optimization_barrier((u, parts[-1][1]))
        increment = products(t, u, loops, row_count)
        pieces = []
        for k in range(cols):
            piece = lax.dynamic_index_in_dim(increment, mine ^ k, 0, keepdims=False)
            if k:
                piece = lax.ppermute(piece, "col", [(i, i ^ k) for i in range(cols)])
            pieces.append(piece)
        parts.append(pieces)
    outs = []
    for t in range(3):
        low, high = (mine & 1) == 1, (mine & 2) == 2
        a, b, c, d = parts[t]
        a, b = jnp.where(low, b, a), jnp.where(low, a, b)
        c, d = jnp.where(low, d, c), jnp.where(low, c, d)
        a, c = jnp.where(high, c, a), jnp.where(high, a, c)
        b, d = jnp.where(high, d, b), jnp.where(high, b, d)
        returned = jnp.stack([a, b, c, d])
        outs.append(
            (vertex[t].astype(jnp.float32) + returned.astype(jnp.float32)).astype(jnp.bfloat16)
        )
    return jnp.stack(outs)


def solution(mesh):
    return jax.shard_map(
        per_device,
        mesh=mesh,
        in_specs=(P(None, "pb", "col", None), P(None, ("pb", "col"), None, None), P(), P()),
        out_specs=P(None, "pb", "col", None),
        check_vma=False,
    )
```

profile of v0, /device:TPU:42, one launch (start us, length us, event | category | flops | bytes accessed | tf_op | source)
XLA Modules:
  0.0 228.8 jit_solution(3454015565978344747)
XLA Ops:
  0.0 1.7 copy-done.2
  1.7 2.7 %shard_map.46 = bf16[64,19,8,128]{3,2,1,0:T(8,128)(2,1)S(1)} custom-call(bf16[3,4,112,896]{3,2,1,0:T(8,128)(2,1)S(1)} %copy-done.2), custom_call_target="tpu_custom_call" | custom-call | tf_op jit(solution)/shard_map/pallas_call | solution.py:194
  4.4 1.5 copy-done.1
  5.9 11.7 %all-to-all-start = ((bf16[64,19,8,128]{3,2,1,0:T(8,128)(2,1)}), bf16[64,19,8,128]{3,2,1,0:T(8,128)(2,1)S(1)}, u32[]{:S(2)}, u32[]{:S(2)}) async-start(bf16[64,19,8,128]{3,2,1,0:T(8,128)(2,1)} %copy-done.1), calls=%async_computation | async-start | bytes 4980736 | tf_op jit(solution)/shard_map/all_to_all | solution.py:370
  17.6 0.1 broadcast_reduce_fusion
  17.8 0.1 broadcast_reduce_fusion.2
  17.9 0.4 fusion.1
  18.4 0.6 reshape.953
  19.0 2.1 fusion.36
  21.2 0.5 copy.34
  21.7 0.1 copy.47
  21.8 1.3 maximum_bitcast_fusion
  23.1 0.1 fusion.5
  23.2 0.5 copy.33
  23.7 0.9 copy.46
  24.6 1.3 copy.38.forward_ref
  25.9 0.1 iota_compare_fusion.3
  26.0 0.1 select_reduce_fusion
  26.2 0.1 fusion.48
  26.3 0.8 reduce-precision_convert_fusion.3
  27.1 0.3 fusion.picks_ref
  27.4 0.5 fusion.14
  27.9 0.1 reduce-precision_convert_fusion.1
  28.0 0.1 reduce-precision_convert_fusion
  28.2 0.1 pad_maximum_fusion.1.wide_ref
  28.3 6.2 %shard_map.47.w_hbm = f32[6,256,896]{2,1,0:T(8,128)S(1)} custom-call(bf16[7,256,256]{2,1,0:T(8,128)(2,1)S(1)} %fusion.picks_ref, bf16[256,2304]{1,0:T(8,128)(2,1)S(1)} %pad_maximum_fusion.1.wide_ref), custom_call_target="tpu_custom_call" | custom-call | tf_op jit(solution)/shard_map/pallas_call | solution.py:83
  34.5 2.4 %copy-done = f32[6,256,896]{2,1,0:T(8,128)} copy-done((f32[6,256,896]{2,1,0:T(8,128)}, f32[6,256,896]{2,1,0:T(8,128)S(1)}, u32[]{:S(2)}) %copy-start) | copy-done | bytes 5505048
  36.9 36.3 %all-to-all-done.x_ref = bf16[64,19,8,128]{3,2,1,0:T(8,128)(2,1)S(1)} async-done(((bf16[64,19,8,128]{3,2,1,0:T(8,128)(2,1)}), bf16[64,19,8,128]{3,2,1,0:T(8,128)(2,1)S(1)}, u32[]{:S(2)}, u32[]{:S(2)}) %all-to-all-start) | async-done | bytes 2490400 | tf_op jit(solution)/shard_map/all_to_all | solution.py:370
  73.3 7.9 %shard_map.48 = bf16[19,512,128]{2,1,0:T(8,128)(2,1)S(1)} custom-call(bf16[64,19,8,128]{3,2,1,0:T(8,128)(2,1)S(1)} %all-to-all-done.x_ref, bf16[512,512]{1,0:T(8,128)(2,1)S(1)} %copy.38.forward_ref, bf16[512,512]{1,0:T(8,128)(2,1)S(1)} %bitcast.136, f32[6,256,896]{2,1,0:T(8,128)} %copy-done), custom_call_target="tpu_custom_call" | custom-call | tf_op jit(solution)/shard_map/pallas_call | solution.py:279
  81.2 3.2 %copy.51 = bf16[19,256,2,128]{3,2,0,1:T(2,128)(2,1)} copy(bf16[19,256,2,128]{3,2,1,0:T(2,128)(2,1)S(1)} %bitcast.135) | data formatting | bytes 4980736 | tf_op jit(solution)/shard_map/reshape | solution.py:395
  84.4 13.1 %all-to-all-start.1 = ((bf16[256,19,2,128]{3,2,1,0:T(2,128)(2,1)}), bf16[256,19,2,128]{3,2,1,0:T(2,128)(2,1)}, u32[]{:S(2)}, u32[]{:S(2)}) async-start(bf16[256,19,2,128]{3,2,1,0:T(2,128)(2,1)} %bitcast.131), calls=%async_computation.1 | async-start | bytes 4980736 | tf_op jit(solution)/shard_map/all_to_all | solution.py:396
  97.5 7.7 %reshape.956 = bf16[3,448,2,4,112]{4,3,2,1,0:T(4,128)(2,1)S(1)} reshape(bf16[3,1,448,896]{3,2,1,0:T(8,128)(2,1)} %param.5) | data formatting | bytes 4816896 | tf_op jit(solution)/shard_map/reshape | solution.py:382
  105.2 0.9 copy.42
  106.2 3.0 %pad.4 = bf16[3,448,2,4,128]{4,3,1,0,2:T(4,128)(2,1)} pad(bf16[3,448,2,4,112]{4,3,1,0,2:T(4,128)(2,1)S(1)} %copy.42, bf16[]{:T(256)} %constant.228.clone.1), padding=0_0x0_0x0_0x0_0x0_16 | pad | bytes 5160962 | tf_op jit(solution)/shard_map/jit(_pad)/pad | solution.py:383
  109.2 4.4 %reshape.957 = bf16[3,448,2,512]{3,1,0,2:T(8,128)(2,1)S(1)} reshape(bf16[3,448,2,4,128]{4,3,1,0,2:T(4,128)(2,1)} %pad.4) | data formatting | bytes 5505024 | tf_op jit(solution)/shard_map/reshape | solution.py:383
  113.6 0.1 fusion.73
  113.7 0.2 slice_bitcast_fusion
  113.9 3.0 %maximum_maximum_fusion.loop_hbm = bf16[3,896,1024]{2,1,0:T(8,128)(2,1)} fusion(bf16[3,448,512]{2,1,0:T(8,128)(2,1)S(1)} %get-tuple-element.16, bf16[3,448,512]{2,1,0:T(8,128)(2,1)S(1)} %fusion.73, bf16[3,448,512]{2,1,0:T(8,128)(2,1)S(1)} %get-tuple-element.15), kind=kLoop, calls=%fused_computation | loop fusion | flops 22020096 | bytes 9633792 | tf_op jit(solution)/shard_map/concatenate | solution.py:385
  116.9 39.6 %all-to-all-done.1 = bf16[256,19,2,128]{3,2,1,0:T(2,128)(2,1)} async-done(((bf16[256,19,2,128]{3,2,1,0:T(2,128)(2,1)}), bf16[256,19,2,128]{3,2,1,0:T(2,128)(2,1)}, u32[]{:S(2)}, u32[]{:S(2)}) %all-to-all-start.1) | async-done | bytes 2490400 | tf_op jit(solution)/shard_map/all_to_all | solution.py:396
  156.5 2.3 %copy.50 = bf16[64,4,19,2,128]{4,0,1,3,2:T(8,128)(2,1)S(1)} copy(bf16[64,4,19,2,128]{4,3,2,1,0:T(2,128)(2,1)} %bitcast.15) | data formatting | bytes 4980736 | tf_op jit(solution)/shard_map/reshape | solution.py:397
  158.9 3.9 %shard_map.49 = bf16[4,112,896]{2,1,0:T(8,128)(2,1)S(1)} custom-call(bf16[19,2,4,64,128]{4,3,2,1,0:T(8,128)(2,1)S(1)} %bitcast.132, bf16[3,896,1024]{2,1,0:T(8,128)(2,1)} %maximum_maximum_fusion.loop_hbm), custom_call_target="tpu_custom_call" | custom-call | tf_op jit(solution)/shard_map/pallas_call | solution.py:345
  162.7 0.8 dynamic-slice_bitcast_fusion.8
  163.6 0.7 collective-permute-start.2
  164.2 1.2 collective-permute-start
  165.4 4.3 %collective-permute-start.1 = (bf16[112,896]{1,0:T(8,128)(2,1)}, bf16[112,896]{1,0:T(8,128)(2,1)}, u32[]{:S(2)}, u32[]{:S(2)}) collective-permute-start(bf16[112,896]{1,0:T(8,128)(2,1)} %get-tuple-element.34), channel_id=1, source_target_pairs={{0,2},{1,3},{2,0},{3,1},{4,6},{5,7},{6,4},{7,5},{8,10},{9,11},{10,... | collective-permute-start | bytes 602120 | tf_op jit(solution)/shard_map/ppermute | solution.py:408
  169.8 3.9 %shard_map.50 = bf16[4,112,896]{2,1,0:T(8,128)(2,1)S(1)} custom-call(bf16[19,2,4,64,128]{4,3,2,1,0:T(8,128)(2,1)S(1)} %bitcast.133, bf16[3,896,1024]{2,1,0:T(8,128)(2,1)} %maximum_maximum_fusion.loop_hbm), custom_call_target="tpu_custom_call" | custom-call | tf_op jit(solution)/shard_map/pallas_call | solution.py:345
  173.6 0.1 dynamic-slice_bitcast_fusion.5
  173.7 0.3 collective-permute-start.5
  174.0 1.5 collective-permute-start.3
  175.6 4.3 %collective-permute-start.4 = (bf16[112,896]{1,0:T(8,128)(2,1)S(1)}, bf16[112,896]{1,0:T(8,128)(2,1)S(1)}, u32[]{:S(2)}, u32[]{:S(2)}) collective-permute-start(bf16[112,896]{1,0:T(8,128)(2,1)S(1)} %get-tuple-element.37), channel_id=1, source_target_pairs={{0,2},{1,3},{2,0},{3,1},{4,6},{5,7},{6,4},{7,5},{8,10},{9,11},{10,... | collective-permute-start | bytes 602120 | tf_op jit(solution)/shard_map/ppermute | solution.py:408
  179.8 11.7 %collective-permute-done = bf16[112,896]{1,0:T(8,128)(2,1)} collective-permute-done((bf16[112,896]{1,0:T(8,128)(2,1)}, bf16[112,896]{1,0:T(8,128)(2,1)}, u32[]{:S(2)}, u32[]{:S(2)}) %collective-permute-start) | collective-permute-done | bytes 200736 | tf_op jit(solution)/shard_map/ppermute | solution.py:408
  191.6 13.9 %collective-permute-done.1 = bf16[112,896]{1,0:T(8,128)(2,1)} collective-permute-done((bf16[112,896]{1,0:T(8,128)(2,1)}, bf16[112,896]{1,0:T(8,128)(2,1)}, u32[]{:S(2)}, u32[]{:S(2)}) %collective-permute-start.1) | collective-permute-done | bytes 200736 | tf_op jit(solution)/shard_map/ppermute | solution.py:408
  205.5 1.1 select_bitcast_fusion.11
  206.7 3.9 %shard_map.51 = bf16[4,112,896]{2,1,0:T(8,128)(2,1)S(1)} custom-call(bf16[19,2,4,64,128]{4,3,2,1,0:T(8,128)(2,1)S(1)} %bitcast.134, bf16[3,896,1024]{2,1,0:T(8,128)(2,1)} %maximum_maximum_fusion.loop_hbm), custom_call_target="tpu_custom_call" | custom-call | tf_op jit(solution)/shard_map/pallas_call | solution.py:345
  210.6 0.1 dynamic-slice_bitcast_fusion
  210.6 0.9 collective-permute-start.6
  211.5 4.9 %collective-permute-start.7 = (bf16[112,896]{1,0:T(8,128)(2,1)S(1)}, bf16[112,896]{1,0:T(8,128)(2,1)S(1)}, u32[]{:S(2)}, u32[]{:S(2)}) collective-permute-start(bf16[112,896]{1,0:T(8,128)(2,1)S(1)} %get-tuple-element.39), channel_id=1, source_target_pairs={{0,2},{1,3},{2,0},{3,1},{4,6},{5,7},{6,4},{7,5},{8,10},{9,11},{10,... | collective-permute-start | bytes 602120 | tf_op jit(solution)/shard_map/ppermute | solution.py:408
  216.4 0.1 collective-permute-start.8
  216.5 0.1 select_bitcast_fusion.7
  216.6 5.0 %collective-permute-done.6 = bf16[112,896]{1,0:T(8,128)(2,1)S(1)} collective-permute-done((bf16[112,896]{1,0:T(8,128)(2,1)S(1)}, bf16[112,896]{1,0:T(8,128)(2,1)S(1)}, u32[]{:S(2)}, u32[]{:S(2)}) %collective-permute-start.6) | collective-permute-done | bytes 200736 | tf_op jit(solution)/shard_map/ppermute | solution.py:408
  221.7 4.6 %collective-permute-done.7 = bf16[112,896]{1,0:T(8,128)(2,1)S(1)} collective-permute-done((bf16[112,896]{1,0:T(8,128)(2,1)S(1)}, bf16[112,896]{1,0:T(8,128)(2,1)S(1)}, u32[]{:S(2)}, u32[]{:S(2)}) %collective-permute-start.7) | collective-permute-done | bytes 200736 | tf_op jit(solution)/shard_map/ppermute | solution.py:408
  226.2 0.1 select_bitcast_fusion.3
  226.4 0.7 add_convert_fusion.2
  227.0 1.7 pad_maximum_fusion
  (36 shorter events, 0.2 us)
Async XLA Ops:
  0.0 1.7 copy-start.2
  4.4 1.5 copy-start.1
  5.9 11.7 %copy-start.5 = (s32[7,3]{0,1:T(4,128)S(1)}, s32[7,3]{0,1:T(4,128)}, u32[]{:S(2)}) copy-start(s32[7,3]{0,1:T(4,128)} %param.7) | copy-start | bytes 256
  5.9 12.0 %copy-start.4 = (f32[6,256]{1,0:T(8,128)S(1)}, f32[6,256]{1,0:T(8,128)}, u32[]{:S(2)}) copy-start(f32[6,256]{1,0:T(8,128)} %param.6) | copy-start | bytes 18436
  5.9 67.4 %all-to-all-start = ((bf16[64,19,8,128]{3,2,1,0:T(8,128)(2,1)}), bf16[64,19,8,128]{3,2,1,0:T(8,128)(2,1)S(1)}, u32[]{:S(2)}, u32[]{:S(2)}) async-start(bf16[64,19,8,128]{3,2,1,0:T(8,128)(2,1)} %copy-done.1), calls=%async_computation | async-start | bytes 4980736 | tf_op jit(solution)/shard_map/all_to_all | solution.py:370
  34.5 2.4 %copy-start = (f32[6,256,896]{2,1,0:T(8,128)}, f32[6,256,896]{2,1,0:T(8,128)S(1)}, u32[]{:S(2)}) copy-start(f32[6,256,896]{2,1,0:T(8,128)S(1)} %shard_map.47.w_hbm) | copy-start | bytes 16515076
  84.4 72.1 %all-to-all-start.1 = ((bf16[256,19,2,128]{3,2,1,0:T(2,128)(2,1)}), bf16[256,19,2,128]{3,2,1,0:T(2,128)(2,1)}, u32[]{:S(2)}, u32[]{:S(2)}) async-start(bf16[256,19,2,128]{3,2,1,0:T(2,128)(2,1)} %bitcast.131), calls=%async_computation.1 | async-start | bytes 4980736 | tf_op jit(solution)/shard_map/all_to_all | solution.py:396
  163.6 6.2 %collective-permute-start.2 = (bf16[112,896]{1,0:T(8,128)(2,1)}, bf16[112,896]{1,0:T(8,128)(2,1)S(1)}, u32[]{:S(2)}, u32[]{:S(2)}) collective-permute-start(bf16[112,896]{1,0:T(8,128)(2,1)} %get-tuple-element.33), channel_id=1, source_target_pairs={{0,1},{1,0},{2,3},{3,2},{4,5},{5,4},{6,7},{7,6},{8,9},{9,8},{10,11... | collective-permute-start | bytes 602120 | tf_op jit(solution)/shard_map/ppermute | solution.py:408
  164.2 27.4 %collective-permute-start = (bf16[112,896]{1,0:T(8,128)(2,1)}, bf16[112,896]{1,0:T(8,128)(2,1)}, u32[]{:S(2)}, u32[]{:S(2)}) collective-permute-start(bf16[112,896]{1,0:T(8,128)(2,1)} %get-tuple-element.32), channel_id=1, source_target_pairs={{0,3},{1,2},{2,1},{3,0},{4,7},{5,6},{6,5},{7,4},{8,11},{9,10},{10,... | collective-permute-start | bytes 602120 | tf_op jit(solution)/shard_map/ppermute | solution.py:408
  165.4 40.1 %collective-permute-start.1 = (bf16[112,896]{1,0:T(8,128)(2,1)}, bf16[112,896]{1,0:T(8,128)(2,1)}, u32[]{:S(2)}, u32[]{:S(2)}) collective-permute-start(bf16[112,896]{1,0:T(8,128)(2,1)} %get-tuple-element.34), channel_id=1, source_target_pairs={{0,2},{1,3},{2,0},{3,1},{4,6},{5,7},{6,4},{7,5},{8,10},{9,11},{10,... | collective-permute-start | bytes 602120 | tf_op jit(solution)/shard_map/ppermute | solution.py:408
  173.7 33.0 %collective-permute-start.5 = (bf16[112,896]{1,0:T(8,128)(2,1)S(1)}, bf16[112,896]{1,0:T(8,128)(2,1)S(1)}, u32[]{:S(2)}, u32[]{:S(2)}) collective-permute-start(bf16[112,896]{1,0:T(8,128)(2,1)S(1)} %get-tuple-element.36), channel_id=1, source_target_pairs={{0,1},{1,0},{2,3},{3,2},{4,5},{5,4},{6,7},{7,6},{8,9},{9,8},{10,11... | collective-permute-start | bytes 602120 | tf_op jit(solution)/shard_map/ppermute | solution.py:408
  174.0 42.5 %collective-permute-start.3 = (bf16[112,896]{1,0:T(8,128)(2,1)S(1)}, bf16[112,896]{1,0:T(8,128)(2,1)S(1)}, u32[]{:S(2)}, u32[]{:S(2)}) collective-permute-start(bf16[112,896]{1,0:T(8,128)(2,1)S(1)} %get-tuple-element.35), channel_id=1, source_target_pairs={{0,3},{1,2},{2,1},{3,0},{4,7},{5,6},{6,5},{7,4},{8,11},{9,10},{10,... | collective-permute-start | bytes 602120 | tf_op jit(solution)/shard_map/ppermute | solution.py:408
  175.6 41.0 %collective-permute-start.4 = (bf16[112,896]{1,0:T(8,128)(2,1)S(1)}, bf16[112,896]{1,0:T(8,128)(2,1)S(1)}, u32[]{:S(2)}, u32[]{:S(2)}) collective-permute-start(bf16[112,896]{1,0:T(8,128)(2,1)S(1)} %get-tuple-element.37), channel_id=1, source_target_pairs={{0,2},{1,3},{2,0},{3,1},{4,6},{5,7},{6,4},{7,5},{8,10},{9,11},{10,... | collective-permute-start | bytes 602120 | tf_op jit(solution)/shard_map/ppermute | solution.py:408
  210.6 15.8 %copy-start.3 = (bf16[3,4,112,896]{3,2,1,0:T(8,128)(2,1)S(1)}, bf16[3,4,112,896]{3,2,1,0:T(8,128)(2,1)}, u32[]{:S(2)}) copy-start(bf16[3,4,112,896]{3,2,1,0:T(8,128)(2,1)} %v_ref.1) | copy-start | bytes 7225348
  210.6 11.0 %collective-permute-start.6 = (bf16[112,896]{1,0:T(8,128)(2,1)S(1)}, bf16[112,896]{1,0:T(8,128)(2,1)S(1)}, u32[]{:S(2)}, u32[]{:S(2)}) collective-permute-start(bf16[112,896]{1,0:T(8,128)(2,1)S(1)} %get-tuple-element.40), channel_id=1, source_target_pairs={{0,3},{1,2},{2,1},{3,0},{4,7},{5,6},{6,5},{7,4},{8,11},{9,10},{10,... | collective-permute-start | bytes 602120 | tf_op jit(solution)/shard_map/ppermute | solution.py:408
  211.5 14.7 %collective-permute-start.7 = (bf16[112,896]{1,0:T(8,128)(2,1)S(1)}, bf16[112,896]{1,0:T(8,128)(2,1)S(1)}, u32[]{:S(2)}, u32[]{:S(2)}) collective-permute-start(bf16[112,896]{1,0:T(8,128)(2,1)S(1)} %get-tuple-element.39), channel_id=1, source_target_pairs={{0,2},{1,3},{2,0},{3,1},{4,6},{5,7},{6,4},{7,5},{8,10},{9,11},{10,... | collective-permute-start | bytes 602120 | tf_op jit(solution)/shard_map/ppermute | solution.py:408
  216.4 9.9 %collective-permute-start.8 = (bf16[112,896]{1,0:T(8,128)(2,1)S(1)}, bf16[112,896]{1,0:T(8,128)(2,1)S(1)}, u32[]{:S(2)}, u32[]{:S(2)}) collective-permute-start(bf16[112,896]{1,0:T(8,128)(2,1)S(1)} %get-tuple-element.38), channel_id=1, source_target_pairs={{0,1},{1,0},{2,3},{3,2},{4,5},{5,4},{6,7},{7,6},{8,9},{9,8},{10,11... | collective-permute-start | bytes 602120 | tf_op jit(solution)/shard_map/ppermute | solution.py:408
where the time goes:
time: 229 us
  waiting for transfers between devices  111 us (48%)
  starting transfers between devices  43 us (19%)
  local copies, waits for them, and re-layouts  32.4 us (14%)
  Pallas kernels  28.5 us (12%)
  other arithmetic  12.3 us (5%)
    all_to_all x1, waiting for transfers between devices, per_device(): lax.all_to_all(united, ('pb', 'col'), split_axis=0, concat_axis=0, tiled=...  39.6 us
    all_to_all x1, waiting for transfers between devices, per_device(): lax.all_to_all(sent, 'pb', split_axis=0, concat_axis=0, tiled=True)  36.3 us
    ppermute x9, waiting for transfers between devices, per_device(): piece = lax.ppermute(piece, 'col', [(i, i ^ k) for i in range(cols)])  35.3 us
    ppermute x9, starting transfers between devices, per_device(): piece = lax.ppermute(piece, 'col', [(i, i ^ k) for i in range(cols)])  18.2 us
    all_to_all x1, starting transfers between devices, per_device(): lax.all_to_all(united, ('pb', 'col'), split_axis=0, concat_axis=0, tiled=...  13.1 us
    all_to_all x1, starting transfers between devices, per_device(): lax.all_to_all(sent, 'pb', split_axis=0, concat_axis=0, tiled=True)  11.7 us
    pallas_call x3, Pallas kernels, products(): pl.pallas_call(functools.partial(products_kernel, t), in_specs=[whole(),...  11.6 us
    reshape x2, local copies, waits for them, and re-layouts, per_device(): loops = loop_blocks.reshape(3, order, 2, cols, row_count)  8.65 us
  transfers between devices with their start and end apart: 11, of which 6 were waited for; matrix products, arithmetic and copies ran while one was open for 14% of the time, Pallas kernels for 6%

commit v1 on v0

--- a/solution.py
+++ b/solution.py
@@ -149,14 +149,22 @@
     return out
 
 
-def spread_kernel(v_ref, out_ref, tmp_ref):
+def spread_kernel(v_hbm, out_hbm, v_ref, tmp_ref, out_ref, in_sems, out_sems):
     channels, mesh_z, row_count, width = v_ref.shape
     groups, tiles, inner, _ = out_ref.shape
     order = width // 2
     narrow = order // groups
-
-    def turn(t, carry):
-        for z in range(mesh_z):
+    share = groups // PARTS
+    arriving = [
+        pltpu.make_async_copy(v_hbm.at[t], v_ref.at[t], in_sems.at[t]) for t in range(channels)
+    ]
+    for copy in arriving:
+        copy.start()
+
+    for t in range(channels):
+        arriving[t].wait()
+
+        def turn(z, carry):
             block = v_ref[t, z].astype(jnp.float32)
             zeros = jnp.zeros((LANES - row_count, width), jnp.float32)
             turned = jnp.concatenate([block, zeros], axis=0).T
@@ -166,21 +174,21 @@
                     tmp_ref[t * narrow + n, pl.ds(2 * z + p, groups, stride=inner), :] = turned[
                         start : start + groups
                     ]
-        return carry
-
-    lax.fori_loop(0, channels, turn, 0)
-    share = groups // PARTS
-
-    def pack(c, carry):
-        rows = pl.ds(pl.multiple_of(c * share * inner, share * inner), share * inner)
+            return carry
+
+        lax.fori_loop(0, mesh_z, turn, 0)
+
+    leaving = []
+    for c in range(PARTS):
+        part = pl.ds(c * share, share)
+        leaving.append(pltpu.make_async_copy(out_ref.at[part], out_hbm.at[part], out_sems.at[c]))
+        rows = pl.ds(c * share * inner, share * inner)
         for j in range(tiles):
-            tile = packed(lambda s, _: tmp_ref[s, rows], j, channels * narrow, row_count)
-            out_ref[pl.ds(c * share, share), j] = tile.reshape(share, inner, LANES).astype(
-                jnp.bfloat16
-            )
-        return carry
-
-    lax.fori_loop(0, PARTS, pack, 0)
+            tile = packed(lambda s, i: tmp_ref[s, rows], j, channels * narrow, row_count)
+            out_ref[part, j] = tile.reshape(share, inner, LANES).astype(jnp.bfloat16)
+        leaving[c].start()
+    for copy in leaving:
+        copy.wait()
 
 
 def whole():
@@ -191,16 +199,21 @@
     channels, mesh_z, row_count, width = vertex.shape
     narrow = width // 2 // groups
     tiles = -(-channels * narrow * row_count // LANES)
+    shape = (groups, tiles, 2 * mesh_z, LANES)
     return pl.pallas_call(
         spread_kernel,
-        in_specs=[whole()],
-        out_specs=whole(),
-        out_shape=jax.ShapeDtypeStruct((groups, tiles, 2 * mesh_z, LANES), jnp.bfloat16),
+        in_specs=[pl.BlockSpec(memory_space=pltpu.HBM)],
+        out_specs=pl.BlockSpec(memory_space=pltpu.HBM),
+        out_shape=pltpu.HBM(shape, jnp.bfloat16),
         scratch_shapes=[
-            pltpu.VMEM((channels * narrow, groups * 2 * mesh_z, LANES), jnp.float32)
+            pltpu.VMEM(vertex.shape, jnp.bfloat16),
+            pltpu.VMEM((channels * narrow, groups * 2 * mesh_z, LANES), jnp.float32),
+            pltpu.VMEM(shape, jnp.bfloat16),
+            pltpu.SemaphoreType.DMA((channels,)),
+            pltpu.SemaphoreType.DMA((PARTS,)),
         ],
         compiler_params=pltpu.CompilerParams(vmem_limit_bytes=32 * 1024 * 1024),
-    )(vertex)
+    )(pltpu.with_memory_space_constraint(vertex, pltpu.HBM))
 
 
 def transform_kernel(
@@ -291,18 +304,21 @@
     )(x, forward, backward, pltpu.with_memory_space_constraint(w, pltpu.HBM))
 
 
-def products_kernel(t, u_ref, loop_hbm, out_ref, loop_ref, tall_ref, wide_ref, sem):
+def products_kernel(t, mine_ref, u_ref, loop_hbm, *refs):
+    out_refs, (loop_ref, tall_ref, wide_ref, sem) = refs[:-4], refs[-4:]
     f32, bf16 = jnp.float32, jnp.bfloat16
+    mine = mine_ref[0]
     tiles, _, cols, groups, _ = u_ref.shape
     order = tall_ref.shape[0] // 2
     narrow = order // groups
     depth = cols * LANES
-    row_count = out_ref.shape[1]
+    row_count = out_refs[0].shape[0]
     copy = pltpu.make_async_copy(loop_hbm.at[t], loop_ref, sem)
     copy.start()
 
     def place(k, carry):
         here = pl.ds(pl.multiple_of(k * LANES, LANES), LANES)
+        slab = pl.ds(pl.multiple_of((k ^ mine) * LANES, LANES), LANES)
         there = pl.ds(pl.multiple_of(depth + k * LANES, LANES), LANES)
         for n in range(narrow):
             real, imag = [
@@ -318,8 +334,8 @@
             real, imag = real.astype(bf16), imag.astype(bf16)
             upper = slice(n * groups, (n + 1) * groups)
             lower = slice(order + n * groups, order + (n + 1) * groups)
-            tall_ref[upper, here] = real
-            tall_ref[lower, here] = imag
+            tall_ref[upper, slab] = real
+            tall_ref[lower, slab] = imag
             wide_ref[upper, here] = real
             wide_ref[upper, there] = minus
             wide_ref[lower, here] = imag
@@ -336,17 +352,21 @@
     )
     increment = (step_length * change).astype(bf16)
     for k in range(cols):
-        out_ref[k] = increment[k * LANES : k * LANES + row_count]
-
-
-def products(t, u, loops, row_count):
+        out_refs[k][...] = increment[k * LANES : k * LANES + row_count]
+
+
+def products(t, mine, u, loops, row_count):
     cols = u.shape[2]
     rows, depth = loops.shape[1:]
     return pl.pallas_call(
         functools.partial(products_kernel, t),
-        in_specs=[whole(), pl.BlockSpec(memory_space=pl.ANY)],
-        out_specs=whole(),
-        out_shape=jax.ShapeDtypeStruct((cols, row_count, rows), jnp.bfloat16),
+        in_specs=[
+            pl.BlockSpec(memory_space=pltpu.SMEM),
+            whole(),
+            pl.BlockSpec(memory_space=pl.ANY),
+        ],
+        out_specs=[whole()] * cols,
+        out_shape=[jax.ShapeDtypeStruct((row_count, rows), jnp.bfloat16)] * cols,
         scratch_shapes=[
             pltpu.VMEM((rows, depth), jnp.bfloat16),
             pltpu.VMEM((rows, depth // 2), jnp.bfloat16),
@@ -354,7 +374,48 @@
             pltpu.SemaphoreType.DMA,
         ],
         compiler_params=pltpu.CompilerParams(vmem_limit_bytes=32 * 1024 * 1024),
-    )(u, pltpu.with_memory_space_constraint(loops, pltpu.HBM))
+    )(mine, u, pltpu.with_memory_space_constraint(loops, pltpu.HBM))
+
+
+def finish_kernel(t, count, mine_ref, v_ref, *refs):
+    piece_refs, out_hbm, (new_ref, sems) = refs[:count], refs[-3], refs[-2:]
+    mine = mine_ref[0]
+    copies = []
+    for k in range(count):
+        q = mine ^ k
+        total = v_ref[0, q].astype(jnp.float32) + piece_refs[k][...].astype(jnp.float32)
+        new_ref[k] = total.astype(jnp.bfloat16)
+        copies.append(pltpu.make_async_copy(new_ref.at[k], out_hbm.at[t, q], sems.at[k]))
+        copies[k].start()
+    for copy in copies:
+        copy.wait()
+
+
+def finish(t, mine, vertex, pieces, out):
+    count = len(pieces)
+    operands = [mine, vertex, *pieces]
+    specs = [
+        pl.BlockSpec(memory_space=pltpu.SMEM),
+        pl.BlockSpec((1,) + vertex.shape[1:], lambda i: (t, 0, 0, 0)),
+    ] + [whole()] * count
+    aliases = {}
+    if out is not None:
+        aliases = {len(operands): 0}
+        operands.append(out)
+        specs.append(pl.BlockSpec(memory_space=pltpu.HBM))
+    return pl.pallas_call(
+        functools.partial(finish_kernel, t, count),
+        grid=(1,),
+        in_specs=specs,
+        out_specs=pl.BlockSpec(memory_space=pltpu.HBM),
+        out_shape=jax.ShapeDtypeStruct(vertex.shape, vertex.dtype),
+        input_output_aliases=aliases,
+        scratch_shapes=[
+            pltpu.VMEM((count,) + vertex.shape[2:], vertex.dtype),
+            pltpu.SemaphoreType.DMA((count,)),
+        ],
+        compiler_params=pltpu.CompilerParams(vmem_limit_bytes=16 * 1024 * 1024),
+    )(*operands)
 
 
 def per_device(vertex, loop_blocks, mixing, bond_offsets):
@@ -395,32 +456,19 @@
     united = united.reshape(tiles, momenta, 2, LANES).transpose(1, 0, 2, 3)
     sent = lax.all_to_all(united, ("pb", "col"), split_axis=0, concat_axis=0, tiled=True)
     u = sent.reshape(groups, cols, tiles, 2, LANES).transpose(2, 3, 1, 0, 4)
-    mine = lax.axis_index("col")
+    mine = lax.axis_index("col").astype(jnp.int32).reshape(1)
     parts = []
     for t in range(3):
         if t:
-            u, parts[-1][1] = lax.optimization_barrier((u, parts[-1][1]))
-        increment = products(t, u, loops, row_count)
-        pieces = []
-        for k in range(cols):
-            piece = lax.dynamic_index_in_dim(increment, mine ^ k, 0, keepdims=False)
-            if k:
-                piece = lax.ppermute(piece, "col", [(i, i ^ k) for i in range(cols)])
-            pieces.append(piece)
+            u, parts[0][1] = lax.optimization_barrier((u, parts[0][1]))
+        pieces = list(products(t, mine, u, loops, row_count))
+        for k in reversed(range(1, cols)):
+            pieces[k] = lax.ppermute(pieces[k], "col", [(i, i ^ k) for i in range(cols)])
         parts.append(pieces)
-    outs = []
+    out = None
     for t in range(3):
-        low, high = (mine & 1) == 1, (mine & 2) == 2
-        a, b, c, d = parts[t]
-        a, b = jnp.where(low, b, a), jnp.where(low, a, b)
-        c, d = jnp.where(low, d, c), jnp.where(low, c, d)
-        a, c = jnp.where(high, c, a), jnp.where(high, a, c)
-        b, d = jnp.where(high, d, b), jnp.where(high, b, d)
-        returned = jnp.stack([a, b, c, d])
-        outs.append(
-            (vertex[t].astype(jnp.float32) + returned.astype(jnp.float32)).astype(jnp.bfloat16)
-        )
-    return jnp.stack(outs)
+        out = finish(t, mine, vertex, parts[t], out)
+    return out
 
 
 def solution(mesh):

time: 229 us -> 228 us (level)
  the two profiles are of different devices: /device:TPU:42 before, /device:TPU:1 now
where the time goes in v1:
time: 228 us; the launch traced here: 227 us
  waiting for transfers between devices  96.5 us (42%)
  starting transfers between devices  42.6 us (19%)
  local copies, waits for them, and re-layouts  40.6 us (18%)
  Pallas kernels  34.3 us (15%)
  other arithmetic  11.8 us (5%)
    all_to_all x1, waiting for transfers between devices, per_device(): lax.all_to_all(united, ('pb', 'col'), split_axis=0, concat_axis=0, tiled=...  42.2 us
    ppermute x9, waiting for transfers between devices, per_device(): lax.ppermute(pieces[k], 'col', [(i, i ^ k) for i in range(cols)])  30.6 us
    all_to_all x1, waiting for transfers between devices, per_device(): lax.all_to_all(sent, 'pb', split_axis=0, concat_axis=0, tiled=True)  23.7 us
    ppermute x9, starting transfers between devices, per_device(): lax.ppermute(pieces[k], 'col', [(i, i ^ k) for i in range(cols)])  19.5 us
    all_to_all x1, starting transfers between devices, per_device(): lax.all_to_all(sent, 'pb', split_axis=0, concat_axis=0, tiled=True)  12.6 us
    pallas_call x3, Pallas kernels, products(): pl.pallas_call(functools.partial(products_kernel, t), in_specs=[pl.BlockS...  11.9 us
    all_to_all x1, starting transfers between devices, per_device(): lax.all_to_all(united, ('pb', 'col'), split_axis=0, concat_axis=0, tiled=...  10.6 us
    add x11, local copies, waits for them, and re-layouts, shifted_slots(): coords[axis][None, :] + sign * bond_offsets[:, axis][:, None]  10.4 us
  transfers between devices with their start and end apart: 11, of which 6 were waited for; matrix products, arithmetic and copies ran while one was open for 20% of the time, Pallas kernels for 7%

profile of v1, /device:TPU:1, one launch (start us, length us, event | category | flops | bytes accessed | tf_op | source)
XLA Modules:
  0.0 227.2 jit_solution(3808477736354305969)
XLA Ops:
  0.0 5.4 %shard_map.46 = bf16[64,19,8,128]{3,2,1,0:T(8,128)(2,1)} custom-call(bf16[3,4,112,896]{3,2,1,0:T(8,128)(2,1)} %v_ref.5), custom_call_target="tpu_custom_call" | custom-call | tf_op jit(solution)/shard_map/pallas_call | solution.py:203
  5.4 12.6 %all-to-all-start = ((bf16[64,19,8,128]{3,2,1,0:T(8,128)(2,1)}), bf16[64,19,8,128]{3,2,1,0:T(8,128)(2,1)S(1)}, u32[]{:S(2)}, u32[]{:S(2)}) async-start(bf16[64,19,8,128]{3,2,1,0:T(8,128)(2,1)} %shard_map.46), calls=%async_computation | async-start | bytes 4980736 | tf_op jit(solution)/shard_map/all_to_all | solution.py:431
  18.0 2.1 fusion.36
  20.3 0.5 copy.35
  21.0 0.2 copy.40.forward_ref
  21.2 1.1 maximum_bitcast_fusion.3
  22.4 1.2 copy.36
  23.6 1.1 copy.49
  24.7 1.4 slice_bitcast_fusion.4
  26.1 0.7 broadcast_reduce_fusion
  26.8 0.7 add.465
  27.5 1.2 add.442
  28.7 1.3 add.457
  30.0 1.3 add.459
  31.3 1.2 add.435
  32.6 1.3 add.452
  33.9 1.4 broadcast_reduce_fusion.2
  35.2 1.3 add.454
  36.5 0.7 reduce-precision_convert_fusion.5
  37.2 0.8 fusion.53
  38.0 0.4 fusion.1
  38.4 0.6 slice_add_fusion.2
  39.0 1.4 reshape.780
  40.6 0.8 select_reduce_fusion
  41.4 0.8 fusion.48
  42.2 0.8 reduce-precision_convert_fusion.3
  43.0 0.3 fusion.picks_ref
  43.3 0.5 fusion.14
  43.8 0.1 reduce-precision_convert_fusion.1
  44.0 0.1 reduce-precision_convert_fusion
  44.2 6.2 %shard_map.47.w_hbm = f32[6,256,896]{2,1,0:T(8,128)S(1)} custom-call(bf16[7,256,256]{2,1,0:T(8,128)(2,1)S(1)} %fusion.picks_ref, bf16[256,2304]{1,0:T(8,128)(2,1)S(1)} %pad_maximum_fusion.wide_ref), custom_call_target="tpu_custom_call" | custom-call | tf_op jit(solution)/shard_map/pallas_call | solution.py:83
  50.4 2.4 %copy-done.1 = f32[6,256,896]{2,1,0:T(8,128)} copy-done((f32[6,256,896]{2,1,0:T(8,128)}, f32[6,256,896]{2,1,0:T(8,128)S(1)}, u32[]{:S(2)}) %copy-start.1) | copy-done | bytes 5505048
  52.8 23.7 %all-to-all-done.x_ref = bf16[64,19,8,128]{3,2,1,0:T(8,128)(2,1)S(1)} async-done(((bf16[64,19,8,128]{3,2,1,0:T(8,128)(2,1)}), bf16[64,19,8,128]{3,2,1,0:T(8,128)(2,1)S(1)}, u32[]{:S(2)}, u32[]{:S(2)}) %all-to-all-start) | async-done | bytes 2490400 | tf_op jit(solution)/shard_map/all_to_all | solution.py:431
  76.5 7.9 %shard_map.48 = bf16[19,512,128]{2,1,0:T(8,128)(2,1)S(1)} custom-call(bf16[64,19,8,128]{3,2,1,0:T(8,128)(2,1)S(1)} %all-to-all-done.x_ref, bf16[512,512]{1,0:T(8,128)(2,1)S(1)} %copy.40.forward_ref, bf16[512,512]{1,0:T(8,128)(2,1)S(1)} %bitcast.62, f32[6,256,896]{2,1,0:T(8,128)} %copy-done.1), custom_call_target="tpu_custom_call" | custom-call | tf_op jit(solution)/shard_map/pallas_call | solution.py:292
  84.4 3.2 %copy.53 = bf16[19,256,2,128]{3,2,0,1:T(2,128)(2,1)} copy(bf16[19,256,2,128]{3,2,1,0:T(2,128)(2,1)S(1)} %bitcast.61) | data formatting | bytes 4980736 | tf_op jit(solution)/shard_map/reshape | solution.py:456
  87.7 10.6 %all-to-all-start.1 = ((bf16[256,19,2,128]{3,2,1,0:T(2,128)(2,1)}), bf16[256,19,2,128]{3,2,1,0:T(2,128)(2,1)}, u32[]{:S(2)}, u32[]{:S(2)}) async-start(bf16[256,19,2,128]{3,2,1,0:T(2,128)(2,1)} %bitcast.57), calls=%async_computation.1 | async-start | bytes 4980736 | tf_op jit(solution)/shard_map/all_to_all | solution.py:457
  98.3 7.7 %reshape.783 = bf16[3,448,2,4,112]{4,3,2,1,0:T(4,128)(2,1)S(1)} reshape(bf16[3,1,448,896]{3,2,1,0:T(8,128)(2,1)} %param.5) | data formatting | bytes 4816896 | tf_op jit(solution)/shard_map/reshape | solution.py:443
  106.0 0.9 copy.44
  106.9 3.0 %pad.4 = bf16[3,448,2,4,128]{4,3,1,0,2:T(4,128)(2,1)} pad(bf16[3,448,2,4,112]{4,3,1,0,2:T(4,128)(2,1)S(1)} %copy.44, bf16[]{:T(256)} %constant.199.clone.1), padding=0_0x0_0x0_0x0_0x0_16 | pad | bytes 5160962 | tf_op jit(solution)/shard_map/jit(_pad)/pad | solution.py:444
  109.9 4.4 %reshape.784 = bf16[3,448,2,512]{3,1,0,2:T(8,128)(2,1)S(1)} reshape(bf16[3,448,2,4,128]{4,3,1,0,2:T(4,128)(2,1)} %pad.4) | data formatting | bytes 5505024 | tf_op jit(solution)/shard_map/reshape | solution.py:444
  114.3 0.1 fusion.73
  114.4 0.2 slice_bitcast_fusion
  114.6 3.0 %maximum_maximum_fusion.loop_hbm = bf16[3,896,1024]{2,1,0:T(8,128)(2,1)} fusion(bf16[3,448,512]{2,1,0:T(8,128)(2,1)S(1)} %get-tuple-element.38, bf16[3,448,512]{2,1,0:T(8,128)(2,1)S(1)} %fusion.73, bf16[3,448,512]{2,1,0:T(8,128)(2,1)S(1)} %get-tuple-element.37), kind=kLoop, calls=%fused_computation | loop fusion | flops 22020096 | bytes 9633792 | tf_op jit(solution)/shard_map/concatenate | solution.py:446
  117.6 42.2 %all-to-all-done.1 = bf16[256,19,2,128]{3,2,1,0:T(2,128)(2,1)} async-done(((bf16[256,19,2,128]{3,2,1,0:T(2,128)(2,1)}), bf16[256,19,2,128]{3,2,1,0:T(2,128)(2,1)}, u32[]{:S(2)}, u32[]{:S(2)}) %all-to-all-start.1) | async-done | bytes 2490400 | tf_op jit(solution)/shard_map/all_to_all | solution.py:457
  159.8 2.3 %copy.52 = bf16[64,4,19,2,128]{4,0,1,3,2:T(8,128)(2,1)S(1)} copy(bf16[64,4,19,2,128]{4,3,2,1,0:T(2,128)(2,1)} %bitcast.16) | data formatting | bytes 4980736 | tf_op jit(solution)/shard_map/reshape | solution.py:458
  162.2 3.9 %shard_map.49 = (bf16[112,896]{1,0:T(8,128)(2,1)S(1)}, bf16[112,896]{1,0:T(8,128)(2,1)S(1)}, bf16[112,896]{1,0:T(8,128)(2,1)S(1)}, bf16[112,896]{1,0:T(8,128)(2,1)S(1)}) custom-call(s32[1]{0:T(128)} %bitcast.mine_ref, bf16[19,2,4,64,128]{4,3,2,1,0:T(8,128)(2,1)S(1)} %bitcast.58, bf16[3,896,1024]{2,1,0:T(8,128)(2,1)} %maximum_maximum_fusion.loop_hbm), custom_call_target="tpu_custom_call" | custom-call | tf_op jit(solution)/shard_map/pallas_call | solution.py:361
  166.1 1.8 collective-permute-start
  167.9 0.5 collective-permute-start.7
  168.4 5.1 %collective-permute-start.8 = (bf16[112,896]{1,0:T(8,128)(2,1)S(1)}, bf16[112,896]{1,0:T(8,128)(2,1)S(1)}, u32[]{:S(2)}, u32[]{:S(2)}) collective-permute-start(bf16[112,896]{1,0:T(8,128)(2,1)S(1)} %get-tuple-element.34), channel_id=1, source_target_pairs={{0,3},{1,2},{2,1},{3,0},{4,7},{5,6},{6,5},{7,4},{8,11},{9,10},{10,... | collective-permute-start | bytes 602120 | tf_op jit(solution)/shard_map/ppermute | solution.py:466
  173.5 3.9 %shard_map.51 = (bf16[112,896]{1,0:T(8,128)(2,1)S(1)}, bf16[112,896]{1,0:T(8,128)(2,1)S(1)}, bf16[112,896]{1,0:T(8,128)(2,1)S(1)}, bf16[112,896]{1,0:T(8,128)(2,1)S(1)}) custom-call(s32[1]{0:T(128)} %bitcast.mine_ref, bf16[19,2,4,64,128]{4,3,2,1,0:T(8,128)(2,1)S(1)} %bitcast.59, bf16[3,896,1024]{2,1,0:T(8,128)(2,1)} %maximum_maximum_fusion.loop_hbm), custom_call_target="tpu_custom_call" | custom-call | tf_op jit(solution)/shard_map/pallas_call | solution.py:361
  177.4 0.5 collective-permute-start.4
  177.9 4.1 %shard_map.50 = (bf16[112,896]{1,0:T(8,128)(2,1)S(1)}, bf16[112,896]{1,0:T(8,128)(2,1)S(1)}, bf16[112,896]{1,0:T(8,128)(2,1)S(1)}, bf16[112,896]{1,0:T(8,128)(2,1)S(1)}) custom-call(s32[1]{0:T(128)} %bitcast.mine_ref, bf16[19,2,4,64,128]{4,3,2,1,0:T(8,128)(2,1)S(1)} %bitcast.60, bf16[3,896,1024]{2,1,0:T(8,128)(2,1)} %maximum_maximum_fusion.loop_hbm), custom_call_target="tpu_custom_call" | custom-call | tf_op jit(solution)/shard_map/pallas_call | solution.py:361
  182.0 0.3 collective-permute-start.1
  182.2 0.5 collective-permute-start.5
  182.7 5.4 %collective-permute-start.6 = (bf16[112,896]{1,0:T(8,128)(2,1)S(1)}, bf16[112,896]{1,0:T(8,128)(2,1)S(1)}, u32[]{:S(2)}, u32[]{:S(2)}) collective-permute-start(bf16[112,896]{1,0:T(8,128)(2,1)S(1)} %get-tuple-element.30), channel_id=1, source_target_pairs={{0,3},{1,2},{2,1},{3,0},{4,7},{5,6},{6,5},{7,4},{8,11},{9,10},{10,... | collective-permute-start | bytes 602120 | tf_op jit(solution)/shard_map/ppermute | solution.py:466
  188.1 0.5 collective-permute-start.2
  188.6 4.9 %collective-permute-start.3 = (bf16[112,896]{1,0:T(8,128)(2,1)S(1)}, bf16[112,896]{1,0:T(8,128)(2,1)S(1)}, u32[]{:S(2)}, u32[]{:S(2)}) collective-permute-start(bf16[112,896]{1,0:T(8,128)(2,1)S(1)} %get-tuple-element.25), channel_id=1, source_target_pairs={{0,3},{1,2},{2,1},{3,0},{4,7},{5,6},{6,5},{7,4},{8,11},{9,10},{10,... | collective-permute-start | bytes 602120 | tf_op jit(solution)/shard_map/ppermute | solution.py:466
  193.6 1.0 shard_map.52.refs_4_
  194.5 7.1 %collective-permute-done.5.refs_2_ = bf16[112,896]{1,0:T(8,128)(2,1)S(1)} collective-permute-done((bf16[112,896]{1,0:T(8,128)(2,1)S(1)}, bf16[112,896]{1,0:T(8,128)(2,1)S(1)}, u32[]{:S(2)}, u32[]{:S(2)}) %collective-permute-start.5) | collective-permute-done | bytes 200736 | tf_op jit(solution)/shard_map/ppermute | solution.py:466
  201.6 11.4 %collective-permute-done.6.refs_3_ = bf16[112,896]{1,0:T(8,128)(2,1)S(1)} collective-permute-done((bf16[112,896]{1,0:T(8,128)(2,1)S(1)}, bf16[112,896]{1,0:T(8,128)(2,1)S(1)}, u32[]{:S(2)}, u32[]{:S(2)}) %collective-permute-start.6) | collective-permute-done | bytes 200736 | tf_op jit(solution)/shard_map/ppermute | solution.py:466
  213.0 1.0 shard_map.53.refs_4_
  213.9 7.8 %collective-permute-done.2.refs_2_ = bf16[112,896]{1,0:T(8,128)(2,1)S(1)} collective-permute-done((bf16[112,896]{1,0:T(8,128)(2,1)S(1)}, bf16[112,896]{1,0:T(8,128)(2,1)S(1)}, u32[]{:S(2)}, u32[]{:S(2)}) %collective-permute-start.2) | collective-permute-done | bytes 200736 | tf_op jit(solution)/shard_map/ppermute | solution.py:466
  221.8 4.3 %collective-permute-done.3.refs_3_ = bf16[112,896]{1,0:T(8,128)(2,1)S(1)} collective-permute-done((bf16[112,896]{1,0:T(8,128)(2,1)S(1)}, bf16[112,896]{1,0:T(8,128)(2,1)S(1)}, u32[]{:S(2)}, u32[]{:S(2)}) %collective-permute-start.3) | collective-permute-done | bytes 200736 | tf_op jit(solution)/shard_map/ppermute | solution.py:466
  226.1 1.0 shard_map.54
  (29 shorter events, 0.5 us)
Async XLA Ops:
  5.4 71.1 %all-to-all-start = ((bf16[64,19,8,128]{3,2,1,0:T(8,128)(2,1)}), bf16[64,19,8,128]{3,2,1,0:T(8,128)(2,1)S(1)}, u32[]{:S(2)}, u32[]{:S(2)}) async-start(bf16[64,19,8,128]{3,2,1,0:T(8,128)(2,1)} %shard_map.46), calls=%async_computation | async-start | bytes 4980736 | tf_op jit(solution)/shard_map/all_to_all | solution.py:431
  18.0 2.9 %copy-start.3 = (s32[256]{0:T(256)}, s32[256]{0:T(256)S(1)}, u32[]{:S(2)}) copy-start(s32[256]{0:T(256)S(1)} %get-tuple-element.64) | copy-start | bytes 3076
  18.0 6.7 %copy-start.2 = (s32[256]{0:T(256)}, s32[256]{0:T(256)S(1)}, u32[]{:S(2)}) copy-start(s32[256]{0:T(256)S(1)} %get-tuple-element.63) | copy-start | bytes 3076
  18.0 2.9 %copy-start.4 = (s32[256]{0:T(256)}, s32[256]{0:T(256)S(1)}, u32[]{:S(2)}) copy-start(s32[256]{0:T(256)S(1)} %and_select_fusion.4) | copy-start | bytes 3076
  50.4 2.4 %copy-start.1 = (f32[6,256,896]{2,1,0:T(8,128)}, f32[6,256,896]{2,1,0:T(8,128)S(1)}, u32[]{:S(2)}) copy-start(f32[6,256,896]{2,1,0:T(8,128)S(1)} %shard_map.47.w_hbm) | copy-start | bytes 16515076
  87.7 72.1 %all-to-all-start.1 = ((bf16[256,19,2,128]{3,2,1,0:T(2,128)(2,1)}), bf16[256,19,2,128]{3,2,1,0:T(2,128)(2,1)}, u32[]{:S(2)}, u32[]{:S(2)}) async-start(bf16[256,19,2,128]{3,2,1,0:T(2,128)(2,1)} %bitcast.57), calls=%async_computation.1 | async-start | bytes 4980736 | tf_op jit(solution)/shard_map/all_to_all | solution.py:457
  166.1 7.5 %collective-permute-start = (bf16[112,896]{1,0:T(8,128)(2,1)S(1)}, bf16[112,896]{1,0:T(8,128)(2,1)S(1)}, u32[]{:S(2)}, u32[]{:S(2)}) collective-permute-start(bf16[112,896]{1,0:T(8,128)(2,1)S(1)} %get-tuple-element.20), channel_id=1, source_target_pairs={{0,1},{1,0},{2,3},{3,2},{4,5},{5,4},{6,7},{7,6},{8,9},{9,8},{10,11... | collective-permute-start | bytes 602120 | tf_op jit(solution)/shard_map/ppermute | solution.py:466
  167.9 14.9 %collective-permute-start.7 = (bf16[112,896]{1,0:T(8,128)(2,1)S(1)}, bf16[112,896]{1,0:T(8,128)(2,1)S(1)}, u32[]{:S(2)}, u32[]{:S(2)}) collective-permute-start(bf16[112,896]{1,0:T(8,128)(2,1)S(1)} %get-tuple-element.33), channel_id=1, source_target_pairs={{0,2},{1,3},{2,0},{3,1},{4,6},{5,7},{6,4},{7,5},{8,10},{9,11},{10,... | collective-permute-start | bytes 602120 | tf_op jit(solution)/shard_map/ppermute | solution.py:466
  168.4 19.7 %collective-permute-start.8 = (bf16[112,896]{1,0:T(8,128)(2,1)S(1)}, bf16[112,896]{1,0:T(8,128)(2,1)S(1)}, u32[]{:S(2)}, u32[]{:S(2)}) collective-permute-start(bf16[112,896]{1,0:T(8,128)(2,1)S(1)} %get-tuple-element.34), channel_id=1, source_target_pairs={{0,3},{1,2},{2,1},{3,0},{4,7},{5,6},{6,5},{7,4},{8,11},{9,10},{10,... | collective-permute-start | bytes 602120 | tf_op jit(solution)/shard_map/ppermute | solution.py:466
  177.4 16.2 %copy-start = (bf16[3,4,112,896]{3,2,1,0:T(8,128)(2,1)S(1)}, bf16[3,4,112,896]{3,2,1,0:T(8,128)(2,1)}, u32[]{:S(2)}) copy-start(bf16[3,4,112,896]{3,2,1,0:T(8,128)(2,1)} %v_ref.5) | copy-start | bytes 7225348
  177.4 11.2 %collective-permute-start.4 = (bf16[112,896]{1,0:T(8,128)(2,1)S(1)}, bf16[112,896]{1,0:T(8,128)(2,1)S(1)}, u32[]{:S(2)}, u32[]{:S(2)}) collective-permute-start(bf16[112,896]{1,0:T(8,128)(2,1)S(1)} %get-tuple-element.28), channel_id=1, source_target_pairs={{0,1},{1,0},{2,3},{3,2},{4,5},{5,4},{6,7},{7,6},{8,9},{9,8},{10,11... | collective-permute-start | bytes 602120 | tf_op jit(solution)/shard_map/ppermute | solution.py:466
  182.0 32.0 %collective-permute-start.1 = (bf16[112,896]{1,0:T(8,128)(2,1)S(1)}, bf16[112,896]{1,0:T(8,128)(2,1)S(1)}, u32[]{:S(2)}, u32[]{:S(2)}) collective-permute-start(bf16[112,896]{1,0:T(8,128)(2,1)S(1)} %get-tuple-element.23), channel_id=1, source_target_pairs={{0,1},{1,0},{2,3},{3,2},{4,5},{5,4},{6,7},{7,6},{8,9},{9,8},{10,11... | collective-permute-start | bytes 602120 | tf_op jit(solution)/shard_map/ppermute | solution.py:466
  182.2 19.4 %collective-permute-start.5 = (bf16[112,896]{1,0:T(8,128)(2,1)S(1)}, bf16[112,896]{1,0:T(8,128)(2,1)S(1)}, u32[]{:S(2)}, u32[]{:S(2)}) collective-permute-start(bf16[112,896]{1,0:T(8,128)(2,1)S(1)} %get-tuple-element.29), channel_id=1, source_target_pairs={{0,2},{1,3},{2,0},{3,1},{4,6},{5,7},{6,4},{7,5},{8,10},{9,11},{10,... | collective-permute-start | bytes 602120 | tf_op jit(solution)/shard_map/ppermute | solution.py:466
  182.7 30.2 %collective-permute-start.6 = (bf16[112,896]{1,0:T(8,128)(2,1)S(1)}, bf16[112,896]{1,0:T(8,128)(2,1)S(1)}, u32[]{:S(2)}, u32[]{:S(2)}) collective-permute-start(bf16[112,896]{1,0:T(8,128)(2,1)S(1)} %get-tuple-element.30), channel_id=1, source_target_pairs={{0,3},{1,2},{2,1},{3,0},{4,7},{5,6},{6,5},{7,4},{8,11},{9,10},{10,... | collective-permute-start | bytes 602120 | tf_op jit(solution)/shard_map/ppermute | solution.py:466
  188.1 33.6 %collective-permute-start.2 = (bf16[112,896]{1,0:T(8,128)(2,1)S(1)}, bf16[112,896]{1,0:T(8,128)(2,1)S(1)}, u32[]{:S(2)}, u32[]{:S(2)}) collective-permute-start(bf16[112,896]{1,0:T(8,128)(2,1)S(1)} %get-tuple-element.24), channel_id=1, source_target_pairs={{0,2},{1,3},{2,0},{3,1},{4,6},{5,7},{6,4},{7,5},{8,10},{9,11},{10,... | collective-permute-start | bytes 602120 | tf_op jit(solution)/shard_map/ppermute | solution.py:466
  188.6 37.4 %collective-permute-start.3 = (bf16[112,896]{1,0:T(8,128)(2,1)S(1)}, bf16[112,896]{1,0:T(8,128)(2,1)S(1)}, u32[]{:S(2)}, u32[]{:S(2)}) collective-permute-start(bf16[112,896]{1,0:T(8,128)(2,1)S(1)} %get-tuple-element.25), channel_id=1, source_target_pairs={{0,3},{1,2},{2,1},{3,0},{4,7},{5,6},{6,5},{7,4},{8,11},{9,10},{10,... | collective-permute-start | bytes 602120 | tf_op jit(solution)/shard_map/ppermute | solution.py:466

commit v2 on v1

--- a/solution.py
+++ b/solution.py
@@ -164,7 +164,7 @@
     for t in range(channels):
         arriving[t].wait()
 
-        def turn(z, carry):
+        for z in range(mesh_z):
             block = v_ref[t, z].astype(jnp.float32)
             zeros = jnp.zeros((LANES - row_count, width), jnp.float32)
             turned = jnp.concatenate([block, zeros], axis=0).T
@@ -174,9 +174,6 @@
                     tmp_ref[t * narrow + n, pl.ds(2 * z + p, groups, stride=inner), :] = turned[
                         start : start + groups
                     ]
-            return carry
-
-        lax.fori_loop(0, mesh_z, turn, 0)
 
     leaving = []
     for c in range(PARTS):
@@ -217,10 +214,11 @@
 
 
 def transform_kernel(
-    length, x_ref, forward_ref, backward_ref, w_hbm, out_ref, lat_ref, mix_ref, w_ref, sem
+    length, x_ref, forward_ref, backward_ref, w_hbm, out_ref, lat_ref, mix_ref, turn_ref, w_ref, sem
 ):
     f32, bf16 = jnp.float32, jnp.bfloat16
     rows = forward_ref.shape[0]
+    momenta = rows // 2
     tiles = x_ref.shape[1]
     spans = -(-length // LANES)
     copy = pltpu.make_async_copy(w_hbm, w_ref, sem)
@@ -234,7 +232,7 @@
             step([2 * i, 2 * i + 1])
             return carry
 
-        lax.fori_loop(0, tiles // 2, pair, 0)
+        lax.fori_loop(0, tiles // 2, pair, 0, unroll=3)
         if tiles % 2:
             step([tiles - 1])
 
@@ -280,8 +278,12 @@
         mixed = jnp.concatenate([mix_ref[j] for j in places], axis=1)
         projected = jnp.dot(backward_ref[...], mixed, preferred_element_type=f32).astype(bf16)
         for place, j in enumerate(places):
-            part = projected[:, place * LANES : (place + 1) * LANES].astype(f32)
-            out_ref[j] = (x_tile(j) + part).astype(bf16)
+            turn_ref[place] = x_tile(j)
+            for p in range(2):
+                half = slice(p * momenta, (p + 1) * momenta)
+                part = projected[half, place * LANES : (place + 1) * LANES].astype(f32)
+                own = turn_ref[place, pl.ds(p, momenta, stride=2), :]
+                out_ref[j, p] = (own + part).astype(bf16)
 
     by_pairs(backward)
 
@@ -293,10 +295,11 @@
         functools.partial(transform_kernel, length),
         in_specs=[whole(), whole(), whole(), pl.BlockSpec(memory_space=pl.ANY)],
         out_specs=whole(),
-        out_shape=jax.ShapeDtypeStruct((tiles, rows, LANES), jnp.bfloat16),
+        out_shape=jax.ShapeDtypeStruct((tiles, 2, rows // 2, LANES), jnp.bfloat16),
         scratch_shapes=[
             pltpu.VMEM((tiles, rows, LANES), jnp.bfloat16),
             pltpu.VMEM((tiles, rows, LANES), jnp.bfloat16),
+            pltpu.VMEM((2, rows, LANES), jnp.float32),
             pltpu.VMEM(w.shape, jnp.float32),
             pltpu.SemaphoreType.DMA,
         ],
@@ -305,16 +308,20 @@
 
 
 def products_kernel(t, mine_ref, u_ref, loop_hbm, *refs):
-    out_refs, (loop_ref, tall_ref, wide_ref, sem) = refs[:-4], refs[-4:]
+    out_refs, (rows_ref, loop_ref, tall_ref, wide_ref, sem) = refs[:-5], refs[-5:]
     f32, bf16 = jnp.float32, jnp.bfloat16
     mine = mine_ref[0]
-    tiles, _, cols, groups, _ = u_ref.shape
+    tiles = rows_ref.shape[0]
+    cols = len(out_refs)
+    groups = u_ref.shape[2] // cols
     order = tall_ref.shape[0] // 2
     narrow = order // groups
     depth = cols * LANES
     row_count = out_refs[0].shape[0]
+    first = t * narrow * row_count // LANES
     copy = pltpu.make_async_copy(loop_hbm.at[t], loop_ref, sem)
     copy.start()
+    rows_ref[...] = u_ref[first : first + tiles].astype(f32)
 
     def place(k, carry):
         here = pl.ds(pl.multiple_of(k * LANES, LANES), LANES)
@@ -323,8 +330,8 @@
         for n in range(narrow):
             real, imag = [
                 cut(
-                    lambda j: u_ref[j, p, k].astype(f32),
-                    (t * narrow + n) * row_count,
+                    lambda j: rows_ref[j, p, pl.ds(k, groups, stride=cols), :],
+                    (t * narrow + n) * row_count - first * LANES,
                     row_count,
                     tiles - 1,
                 )
@@ -356,8 +363,10 @@
 
 
 def products(t, mine, u, loops, row_count):
-    cols = u.shape[2]
     rows, depth = loops.shape[1:]
+    cols = depth // 2 // LANES
+    length = rows // 2 // (u.shape[2] // cols) * row_count
+    tiles = -(-(t + 1) * length // LANES) - t * length // LANES
     return pl.pallas_call(
         functools.partial(products_kernel, t),
         in_specs=[
@@ -368,6 +377,7 @@
         out_specs=[whole()] * cols,
         out_shape=[jax.ShapeDtypeStruct((row_count, rows), jnp.bfloat16)] * cols,
         scratch_shapes=[
+            pltpu.VMEM((tiles,) + u.shape[1:], jnp.float32),
             pltpu.VMEM((rows, depth), jnp.bfloat16),
             pltpu.VMEM((rows, depth // 2), jnp.bfloat16),
             pltpu.VMEM((rows, depth), jnp.bfloat16),
@@ -383,7 +393,7 @@
     copies = []
     for k in range(count):
         q = mine ^ k
-        total = v_ref[0, q].astype(jnp.float32) + piece_refs[k][...].astype(jnp.float32)
+        total = v_ref[t, q].astype(jnp.float32) + piece_refs[k][...].astype(jnp.float32)
         new_ref[k] = total.astype(jnp.bfloat16)
         copies.append(pltpu.make_async_copy(new_ref.at[k], out_hbm.at[t, q], sems.at[k]))
         copies[k].start()
@@ -396,7 +406,7 @@
     operands = [mine, vertex, *pieces]
     specs = [
         pl.BlockSpec(memory_space=pltpu.SMEM),
-        pl.BlockSpec((1,) + vertex.shape[1:], lambda i: (t, 0, 0, 0)),
+        whole(),
     ] + [whole()] * count
     aliases = {}
     if out is not None:
@@ -405,7 +415,6 @@
         specs.append(pl.BlockSpec(memory_space=pltpu.HBM))
     return pl.pallas_call(
         functools.partial(finish_kernel, t, count),
-        grid=(1,),
         in_specs=specs,
         out_specs=pl.BlockSpec(memory_space=pltpu.HBM),
         out_shape=jax.ShapeDtypeStruct(vertex.shape, vertex.dtype),
@@ -432,7 +441,7 @@
 
     forward, backward = phase_tables(momenta, MX, mesh_y, mesh_z)
     forward = forward.transpose(2, 3, 1, 0).reshape(2 * momenta, 2 * momenta)
-    backward = backward.transpose(3, 2, 0, 1).reshape(2 * momenta, 2 * momenta)
+    backward = backward.transpose(2, 3, 0, 1).reshape(2 * momenta, 2 * momenta)
     bond = jnp.arange(NB, dtype=jnp.int32)
     own = (jnp.arange(narrow, dtype=jnp.int32) * groups + lax.axis_index("pb")) % NB
     column_bonds = jnp.sum(
@@ -452,10 +461,9 @@
     )
 
     united = transform(gathered, forward, backward, w, narrow * row_count)
-    tiles = united.shape[0]
-    united = united.reshape(tiles, momenta, 2, LANES).transpose(1, 0, 2, 3)
+    united = united.transpose(2, 0, 1, 3)
     sent = lax.all_to_all(united, ("pb", "col"), split_axis=0, concat_axis=0, tiled=True)
-    u = sent.reshape(groups, cols, tiles, 2, LANES).transpose(2, 3, 1, 0, 4)
+    u = sent.transpose(1, 2, 0, 3)
     mine = lax.axis_index("col").astype(jnp.int32).reshape(1)
     parts = []
     for t in range(3):

time: 228 us -> 227 us (level)
    reshape x2 -> x0, local copies, waits for them, and re-layouts: 5.59 us -> none  [the longest x1 3.24 us: per_device(): united = united.reshape(tiles, momenta, 2, LANES).transpose(1, 0, 2, 3)]
    transpose x1 -> x2, local copies, waits for them, and re-layouts: 1.18 us -> 5.2 us  [the longest x1 4.1 us: per_device(): united = united.transpose(2, 0, 1, 3)]
where the time goes in v2:
time: 227 us; the launch traced here: 226 us
  waiting for transfers between devices  96.4 us (42%)
  starting transfers between devices  42.8 us (19%)
  local copies, waits for them, and re-layouts  41.3 us (18%)
  Pallas kernels  32.1 us (14%)
  other arithmetic  11.8 us (5%)
    all_to_all x1, waiting for transfers between devices, per_device(): lax.all_to_all(united, ('pb', 'col'), split_axis=0, concat_axis=0, tiled=...  42.2 us
    ppermute x9, waiting for transfers between devices, per_device(): lax.ppermute(pieces[k], 'col', [(i, i ^ k) for i in range(cols)])  30.5 us
    all_to_all x1, waiting for transfers between devices, per_device(): lax.all_to_all(sent, 'pb', split_axis=0, concat_axis=0, tiled=True)  23.6 us
    ppermute x9, starting transfers between devices, per_device(): lax.ppermute(pieces[k], 'col', [(i, i ^ k) for i in range(cols)])  19.5 us
    all_to_all x1, starting transfers between devices, per_device(): lax.all_to_all(sent, 'pb', split_axis=0, concat_axis=0, tiled=True)  12.7 us
    pallas_call x3, Pallas kernels, products(): pl.pallas_call(functools.partial(products_kernel, t), in_specs=[pl.BlockS...  11.8 us
    all_to_all x1, starting transfers between devices, per_device(): lax.all_to_all(united, ('pb', 'col'), split_axis=0, concat_axis=0, tiled=...  10.6 us
    add x11, local copies, waits for them, and re-layouts, shifted_slots(): coords[axis][None, :] + sign * bond_offsets[:, axis][:, None]  10.4 us
  transfers between devices with their start and end apart: 11, of which 6 were waited for; matrix products, arithmetic and copies ran while one was open for 20% of the time, Pallas kernels for 7%

profile of v2, /device:TPU:1, one launch (start us, length us, event | category | flops | bytes accessed | tf_op | source)
XLA Modules:
  0.0 225.8 jit_solution(17419236035148976591)
XLA Ops:
  0.0 4.6 %shard_map.46 = bf16[64,19,8,128]{3,2,1,0:T(8,128)(2,1)} custom-call(bf16[3,4,112,896]{3,2,1,0:T(8,128)(2,1)} %v_ref.5), custom_call_target="tpu_custom_call" | custom-call | tf_op jit(solution)/shard_map/pallas_call | solution.py:200
  4.6 12.7 %all-to-all-start = ((bf16[64,19,8,128]{3,2,1,0:T(8,128)(2,1)}), bf16[64,19,8,128]{3,2,1,0:T(8,128)(2,1)S(1)}, u32[]{:S(2)}, u32[]{:S(2)}) async-start(bf16[64,19,8,128]{3,2,1,0:T(8,128)(2,1)} %shard_map.46), calls=%async_computation | async-start | bytes 4980736 | tf_op jit(solution)/shard_map/all_to_all | solution.py:440
  17.4 2.1 fusion.36
  19.7 0.5 copy.32
  20.3 0.2 copy.37.forward_ref
  20.5 1.1 maximum_bitcast_fusion.3
  21.7 1.1 copy.33
  22.9 1.1 copy.43
  24.0 1.4 slice_bitcast_fusion.4
  25.4 0.7 broadcast_reduce_fusion
  26.1 0.7 add.465
  26.8 1.2 add.442
  28.0 1.3 add.457
  29.3 1.3 add.459
  30.6 1.2 add.435
  31.8 1.3 add.452
  33.1 1.4 broadcast_reduce_fusion.2
  34.5 1.3 add.454
  35.8 0.7 reduce-precision_convert_fusion.5
  36.5 0.8 fusion.53
  37.3 0.4 fusion.1
  37.6 0.6 slice_add_fusion.2
  38.3 1.4 reshape.774
  39.9 0.8 select_reduce_fusion
  40.7 0.8 fusion.48
  41.5 0.8 reduce-precision_convert_fusion.3
  42.3 0.3 fusion.picks_ref
  42.6 0.5 fusion.14
  43.1 0.1 reduce-precision_convert_fusion.1
  43.2 0.1 reduce-precision_convert_fusion
  43.5 6.2 %shard_map.47.w_hbm = f32[6,256,896]{2,1,0:T(8,128)S(1)} custom-call(bf16[7,256,256]{2,1,0:T(8,128)(2,1)S(1)} %fusion.picks_ref, bf16[256,2304]{1,0:T(8,128)(2,1)S(1)} %pad_maximum_fusion.wide_ref), custom_call_target="tpu_custom_call" | custom-call | tf_op jit(solution)/shard_map/pallas_call | solution.py:83
  49.7 2.4 %copy-done.1 = f32[6,256,896]{2,1,0:T(8,128)} copy-done((f32[6,256,896]{2,1,0:T(8,128)}, f32[6,256,896]{2,1,0:T(8,128)S(1)}, u32[]{:S(2)}) %copy-start.1) | copy-done | bytes 5505048
  52.1 23.6 %all-to-all-done.x_ref = bf16[64,19,8,128]{3,2,1,0:T(8,128)(2,1)S(1)} async-done(((bf16[64,19,8,128]{3,2,1,0:T(8,128)(2,1)}), bf16[64,19,8,128]{3,2,1,0:T(8,128)(2,1)S(1)}, u32[]{:S(2)}, u32[]{:S(2)}) %all-to-all-start) | async-done | bytes 2490400 | tf_op jit(solution)/shard_map/all_to_all | solution.py:440
  75.7 6.6 %shard_map.48 = bf16[19,2,256,128]{3,2,1,0:T(8,128)(2,1)S(1)} custom-call(bf16[64,19,8,128]{3,2,1,0:T(8,128)(2,1)S(1)} %all-to-all-done.x_ref, bf16[512,512]{1,0:T(8,128)(2,1)S(1)} %copy.37.forward_ref, bf16[512,512]{1,0:T(8,128)(2,1)S(1)} %bitcast.58, f32[6,256,896]{2,1,0:T(8,128)} %copy-done.1), custom_call_target="tpu_custom_call" | custom-call | tf_op jit(solution)/shard_map/pallas_call | solution.py:294
  82.3 4.1 %copy.38 = bf16[256,19,2,128]{3,2,1,0:T(2,128)(2,1)} copy(bf16[256,19,2,128]{3,0,2,1:T(8,128)(2,1)S(1)} %bitcast.57) | data formatting | bytes 4980736 | tf_op jit(solution)/shard_map/transpose | solution.py:464
  86.4 10.6 %all-to-all-start.1 = ((bf16[256,19,2,128]{3,2,1,0:T(2,128)(2,1)}), bf16[256,19,2,128]{3,2,1,0:T(2,128)(2,1)}, u32[]{:S(2)}, u32[]{:S(2)}) async-start(bf16[256,19,2,128]{3,2,1,0:T(2,128)(2,1)} %copy.38), calls=%async_computation.1 | async-start | bytes 4980736 | tf_op jit(solution)/shard_map/all_to_all | solution.py:465
  97.0 7.7 %reshape.775 = bf16[3,448,2,4,112]{4,3,2,1,0:T(4,128)(2,1)S(1)} reshape(bf16[3,1,448,896]{3,2,1,0:T(8,128)(2,1)} %param.5) | data formatting | bytes 4816896 | tf_op jit(solution)/shard_map/reshape | solution.py:452
  104.7 0.9 copy.40
  105.6 3.0 %pad.4 = bf16[3,448,2,4,128]{4,3,1,0,2:T(4,128)(2,1)} pad(bf16[3,448,2,4,112]{4,3,1,0,2:T(4,128)(2,1)S(1)} %copy.40, bf16[]{:T(256)} %constant.199.clone.1), padding=0_0x0_0x0_0x0_0x0_16 | pad | bytes 5160962 | tf_op jit(solution)/shard_map/jit(_pad)/pad | solution.py:453
  108.6 4.4 %reshape.776 = bf16[3,448,2,512]{3,1,0,2:T(8,128)(2,1)S(1)} reshape(bf16[3,448,2,4,128]{4,3,1,0,2:T(4,128)(2,1)} %pad.4) | data formatting | bytes 5505024 | tf_op jit(solution)/shard_map/reshape | solution.py:453
  113.0 0.1 fusion.73
  113.1 0.2 slice_bitcast_fusion
  113.3 3.0 %maximum_maximum_fusion.loop_hbm = bf16[3,896,1024]{2,1,0:T(8,128)(2,1)} fusion(bf16[3,448,512]{2,1,0:T(8,128)(2,1)S(1)} %get-tuple-element.38, bf16[3,448,512]{2,1,0:T(8,128)(2,1)S(1)} %fusion.73, bf16[3,448,512]{2,1,0:T(8,128)(2,1)S(1)} %get-tuple-element.37), kind=kLoop, calls=%fused_computation | loop fusion | flops 22020096 | bytes 9633792 | tf_op jit(solution)/shard_map/concatenate | solution.py:455
  116.3 42.2 %all-to-all-done.1 = bf16[256,19,2,128]{3,2,1,0:T(2,128)(2,1)} async-done(((bf16[256,19,2,128]{3,2,1,0:T(2,128)(2,1)}), bf16[256,19,2,128]{3,2,1,0:T(2,128)(2,1)}, u32[]{:S(2)}, u32[]{:S(2)}) %all-to-all-start.1) | async-done | bytes 2490400 | tf_op jit(solution)/shard_map/all_to_all | solution.py:465
  158.5 2.3 %copy.45 = bf16[256,19,2,128]{3,0,2,1:T(8,128)(2,1)S(1)} copy(bf16[256,19,2,128]{3,2,1,0:T(2,128)(2,1)} %all-to-all-done.1) | data formatting | bytes 4980736 | tf_op jit(solution)/shard_map/all_to_all | solution.py:465
  160.8 3.9 %shard_map.49 = (bf16[112,896]{1,0:T(8,128)(2,1)S(1)}, bf16[112,896]{1,0:T(8,128)(2,1)S(1)}, bf16[112,896]{1,0:T(8,128)(2,1)S(1)}, bf16[112,896]{1,0:T(8,128)(2,1)S(1)}) custom-call(s32[1]{0:T(128)} %bitcast.mine_ref, bf16[19,2,256,128]{3,2,1,0:T(8,128)(2,1)S(1)} %bitcast.54, bf16[3,896,1024]{2,1,0:T(8,128)(2,1)} %maximum_maximum_fusion.loop_hbm), custom_call_target="tpu_custom_call" | custom-call | tf_op jit(solution)/shard_map/pallas_call | solution.py:370
  164.7 1.8 collective-permute-start
  166.5 0.5 collective-permute-start.7
  167.0 5.1 %collective-permute-start.8 = (bf16[112,896]{1,0:T(8,128)(2,1)S(1)}, bf16[112,896]{1,0:T(8,128)(2,1)S(1)}, u32[]{:S(2)}, u32[]{:S(2)}) collective-permute-start(bf16[112,896]{1,0:T(8,128)(2,1)S(1)} %get-tuple-element.34), channel_id=1, source_target_pairs={{0,3},{1,2},{2,1},{3,0},{4,7},{5,6},{6,5},{7,4},{8,11},{9,10},{10,... | collective-permute-start | bytes 602120 | tf_op jit(solution)/shard_map/ppermute | solution.py:474
  172.1 3.9 %shard_map.51 = (bf16[112,896]{1,0:T(8,128)(2,1)S(1)}, bf16[112,896]{1,0:T(8,128)(2,1)S(1)}, bf16[112,896]{1,0:T(8,128)(2,1)S(1)}, bf16[112,896]{1,0:T(8,128)(2,1)S(1)}) custom-call(s32[1]{0:T(128)} %bitcast.mine_ref, bf16[19,2,256,128]{3,2,1,0:T(8,128)(2,1)S(1)} %bitcast.55, bf16[3,896,1024]{2,1,0:T(8,128)(2,1)} %maximum_maximum_fusion.loop_hbm), custom_call_target="tpu_custom_call" | custom-call | tf_op jit(solution)/shard_map/pallas_call | solution.py:370
  176.0 0.5 collective-permute-start.4
  176.5 4.1 %shard_map.50 = (bf16[112,896]{1,0:T(8,128)(2,1)S(1)}, bf16[112,896]{1,0:T(8,128)(2,1)S(1)}, bf16[112,896]{1,0:T(8,128)(2,1)S(1)}, bf16[112,896]{1,0:T(8,128)(2,1)S(1)}) custom-call(s32[1]{0:T(128)} %bitcast.mine_ref, bf16[19,2,256,128]{3,2,1,0:T(8,128)(2,1)S(1)} %bitcast.56, bf16[3,896,1024]{2,1,0:T(8,128)(2,1)} %maximum_maximum_fusion.loop_hbm), custom_call_target="tpu_custom_call" | custom-call | tf_op jit(solution)/shard_map/pallas_call | solution.py:370
  180.6 0.3 collective-permute-start.1
  180.9 0.5 collective-permute-start.5
  181.4 5.4 %collective-permute-start.6 = (bf16[112,896]{1,0:T(8,128)(2,1)S(1)}, bf16[112,896]{1,0:T(8,128)(2,1)S(1)}, u32[]{:S(2)}, u32[]{:S(2)}) collective-permute-start(bf16[112,896]{1,0:T(8,128)(2,1)S(1)} %get-tuple-element.30), channel_id=1, source_target_pairs={{0,3},{1,2},{2,1},{3,0},{4,7},{5,6},{6,5},{7,4},{8,11},{9,10},{10,... | collective-permute-start | bytes 602120 | tf_op jit(solution)/shard_map/ppermute | solution.py:474
  186.8 0.5 collective-permute-start.2
  187.3 4.9 %collective-permute-start.3 = (bf16[112,896]{1,0:T(8,128)(2,1)S(1)}, bf16[112,896]{1,0:T(8,128)(2,1)S(1)}, u32[]{:S(2)}, u32[]{:S(2)}) collective-permute-start(bf16[112,896]{1,0:T(8,128)(2,1)S(1)} %get-tuple-element.25), channel_id=1, source_target_pairs={{0,3},{1,2},{2,1},{3,0},{4,7},{5,6},{6,5},{7,4},{8,11},{9,10},{10,... | collective-permute-start | bytes 602120 | tf_op jit(solution)/shard_map/ppermute | solution.py:474
  192.2 1.0 shard_map.52.refs_4_
  193.2 7.0 %collective-permute-done.5.refs_2_ = bf16[112,896]{1,0:T(8,128)(2,1)S(1)} collective-permute-done((bf16[112,896]{1,0:T(8,128)(2,1)S(1)}, bf16[112,896]{1,0:T(8,128)(2,1)S(1)}, u32[]{:S(2)}, u32[]{:S(2)}) %collective-permute-start.5) | collective-permute-done | bytes 200736 | tf_op jit(solution)/shard_map/ppermute | solution.py:474
  200.2 11.4 %collective-permute-done.6.refs_3_ = bf16[112,896]{1,0:T(8,128)(2,1)S(1)} collective-permute-done((bf16[112,896]{1,0:T(8,128)(2,1)S(1)}, bf16[112,896]{1,0:T(8,128)(2,1)S(1)}, u32[]{:S(2)}, u32[]{:S(2)}) %collective-permute-start.6) | collective-permute-done | bytes 200736 | tf_op jit(solution)/shard_map/ppermute | solution.py:474
  211.6 1.0 shard_map.53.refs_4_
  212.5 7.8 %collective-permute-done.2.refs_2_ = bf16[112,896]{1,0:T(8,128)(2,1)S(1)} collective-permute-done((bf16[112,896]{1,0:T(8,128)(2,1)S(1)}, bf16[112,896]{1,0:T(8,128)(2,1)S(1)}, u32[]{:S(2)}, u32[]{:S(2)}) %collective-permute-start.2) | collective-permute-done | bytes 200736 | tf_op jit(solution)/shard_map/ppermute | solution.py:474
  220.4 4.3 %collective-permute-done.3.refs_3_ = bf16[112,896]{1,0:T(8,128)(2,1)S(1)} collective-permute-done((bf16[112,896]{1,0:T(8,128)(2,1)S(1)}, bf16[112,896]{1,0:T(8,128)(2,1)S(1)}, u32[]{:S(2)}, u32[]{:S(2)}) %collective-permute-start.3) | collective-permute-done | bytes 200736 | tf_op jit(solution)/shard_map/ppermute | solution.py:474
  224.7 1.0 shard_map.54
  (29 shorter events, 0.5 us)
Async XLA Ops:
  4.6 71.1 %all-to-all-start = ((bf16[64,19,8,128]{3,2,1,0:T(8,128)(2,1)}), bf16[64,19,8,128]{3,2,1,0:T(8,128)(2,1)S(1)}, u32[]{:S(2)}, u32[]{:S(2)}) async-start(bf16[64,19,8,128]{3,2,1,0:T(8,128)(2,1)} %shard_map.46), calls=%async_computation | async-start | bytes 4980736 | tf_op jit(solution)/shard_map/all_to_all | solution.py:440
  17.3 2.9 %copy-start.3 = (s32[256]{0:T(256)}, s32[256]{0:T(256)S(1)}, u32[]{:S(2)}) copy-start(s32[256]{0:T(256)S(1)} %get-tuple-element.64) | copy-start | bytes 3076
  17.3 6.6 %copy-start.2 = (s32[256]{0:T(256)}, s32[256]{0:T(256)S(1)}, u32[]{:S(2)}) copy-start(s32[256]{0:T(256)S(1)} %get-tuple-element.63) | copy-start | bytes 3076
  17.4 2.9 %copy-start.4 = (s32[256]{0:T(256)}, s32[256]{0:T(256)S(1)}, u32[]{:S(2)}) copy-start(s32[256]{0:T(256)S(1)} %and_select_fusion.4) | copy-start | bytes 3076
  49.7 2.4 %copy-start.1 = (f32[6,256,896]{2,1,0:T(8,128)}, f32[6,256,896]{2,1,0:T(8,128)S(1)}, u32[]{:S(2)}) copy-start(f32[6,256,896]{2,1,0:T(8,128)S(1)} %shard_map.47.w_hbm) | copy-start | bytes 16515076
  86.4 72.1 %all-to-all-start.1 = ((bf16[256,19,2,128]{3,2,1,0:T(2,128)(2,1)}), bf16[256,19,2,128]{3,2,1,0:T(2,128)(2,1)}, u32[]{:S(2)}, u32[]{:S(2)}) async-start(bf16[256,19,2,128]{3,2,1,0:T(2,128)(2,1)} %copy.38), calls=%async_computation.1 | async-start | bytes 4980736 | tf_op jit(solution)/shard_map/all_to_all | solution.py:465
  164.7 7.5 %collective-permute-start = (bf16[112,896]{1,0:T(8,128)(2,1)S(1)}, bf16[112,896]{1,0:T(8,128)(2,1)S(1)}, u32[]{:S(2)}, u32[]{:S(2)}) collective-permute-start(bf16[112,896]{1,0:T(8,128)(2,1)S(1)} %get-tuple-element.20), channel_id=1, source_target_pairs={{0,1},{1,0},{2,3},{3,2},{4,5},{5,4},{6,7},{7,6},{8,9},{9,8},{10,11... | collective-permute-start | bytes 602120 | tf_op jit(solution)/shard_map/ppermute | solution.py:474
  166.5 14.9 %collective-permute-start.7 = (bf16[112,896]{1,0:T(8,128)(2,1)S(1)}, bf16[112,896]{1,0:T(8,128)(2,1)S(1)}, u32[]{:S(2)}, u32[]{:S(2)}) collective-permute-start(bf16[112,896]{1,0:T(8,128)(2,1)S(1)} %get-tuple-element.33), channel_id=1, source_target_pairs={{0,2},{1,3},{2,0},{3,1},{4,6},{5,7},{6,4},{7,5},{8,10},{9,11},{10,... | collective-permute-start | bytes 602120 | tf_op jit(solution)/shard_map/ppermute | solution.py:474
  167.0 19.8 %collective-permute-start.8 = (bf16[112,896]{1,0:T(8,128)(2,1)S(1)}, bf16[112,896]{1,0:T(8,128)(2,1)S(1)}, u32[]{:S(2)}, u32[]{:S(2)}) collective-permute-start(bf16[112,896]{1,0:T(8,128)(2,1)S(1)} %get-tuple-element.34), channel_id=1, source_target_pairs={{0,3},{1,2},{2,1},{3,0},{4,7},{5,6},{6,5},{7,4},{8,11},{9,10},{10,... | collective-permute-start | bytes 602120 | tf_op jit(solution)/shard_map/ppermute | solution.py:474
  176.0 16.2 %copy-start = (bf16[3,4,112,896]{3,2,1,0:T(8,128)(2,1)S(1)}, bf16[3,4,112,896]{3,2,1,0:T(8,128)(2,1)}, u32[]{:S(2)}) copy-start(bf16[3,4,112,896]{3,2,1,0:T(8,128)(2,1)} %v_ref.5) | copy-start | bytes 7225348
  176.0 11.2 %collective-permute-start.4 = (bf16[112,896]{1,0:T(8,128)(2,1)S(1)}, bf16[112,896]{1,0:T(8,128)(2,1)S(1)}, u32[]{:S(2)}, u32[]{:S(2)}) collective-permute-start(bf16[112,896]{1,0:T(8,128)(2,1)S(1)} %get-tuple-element.28), channel_id=1, source_target_pairs={{0,1},{1,0},{2,3},{3,2},{4,5},{5,4},{6,7},{7,6},{8,9},{9,8},{10,11... | collective-permute-start | bytes 602120 | tf_op jit(solution)/shard_map/ppermute | solution.py:474
  180.6 31.9 %collective-permute-start.1 = (bf16[112,896]{1,0:T(8,128)(2,1)S(1)}, bf16[112,896]{1,0:T(8,128)(2,1)S(1)}, u32[]{:S(2)}, u32[]{:S(2)}) collective-permute-start(bf16[112,896]{1,0:T(8,128)(2,1)S(1)} %get-tuple-element.23), channel_id=1, source_target_pairs={{0,1},{1,0},{2,3},{3,2},{4,5},{5,4},{6,7},{7,6},{8,9},{9,8},{10,11... | collective-permute-start | bytes 602120 | tf_op jit(solution)/shard_map/ppermute | solution.py:474
  180.9 19.3 %collective-permute-start.5 = (bf16[112,896]{1,0:T(8,128)(2,1)S(1)}, bf16[112,896]{1,0:T(8,128)(2,1)S(1)}, u32[]{:S(2)}, u32[]{:S(2)}) collective-permute-start(bf16[112,896]{1,0:T(8,128)(2,1)S(1)} %get-tuple-element.29), channel_id=1, source_target_pairs={{0,2},{1,3},{2,0},{3,1},{4,6},{5,7},{6,4},{7,5},{8,10},{9,11},{10,... | collective-permute-start | bytes 602120 | tf_op jit(solution)/shard_map/ppermute | solution.py:474
  181.4 30.2 %collective-permute-start.6 = (bf16[112,896]{1,0:T(8,128)(2,1)S(1)}, bf16[112,896]{1,0:T(8,128)(2,1)S(1)}, u32[]{:S(2)}, u32[]{:S(2)}) collective-permute-start(bf16[112,896]{1,0:T(8,128)(2,1)S(1)} %get-tuple-element.30), channel_id=1, source_target_pairs={{0,3},{1,2},{2,1},{3,0},{4,7},{5,6},{6,5},{7,4},{8,11},{9,10},{10,... | collective-permute-start | bytes 602120 | tf_op jit(solution)/shard_map/ppermute | solution.py:474
  186.8 33.6 %collective-permute-start.2 = (bf16[112,896]{1,0:T(8,128)(2,1)S(1)}, bf16[112,896]{1,0:T(8,128)(2,1)S(1)}, u32[]{:S(2)}, u32[]{:S(2)}) collective-permute-start(bf16[112,896]{1,0:T(8,128)(2,1)S(1)} %get-tuple-element.24), channel_id=1, source_target_pairs={{0,2},{1,3},{2,0},{3,1},{4,6},{5,7},{6,4},{7,5},{8,10},{9,11},{10,... | collective-permute-start | bytes 602120 | tf_op jit(solution)/shard_map/ppermute | solution.py:474
  187.3 37.4 %collective-permute-start.3 = (bf16[112,896]{1,0:T(8,128)(2,1)S(1)}, bf16[112,896]{1,0:T(8,128)(2,1)S(1)}, u32[]{:S(2)}, u32[]{:S(2)}) collective-permute-start(bf16[112,896]{1,0:T(8,128)(2,1)S(1)} %get-tuple-element.25), channel_id=1, source_target_pairs={{0,3},{1,2},{2,1},{3,0},{4,7},{5,6},{6,5},{7,4},{8,11},{9,10},{10,... | collective-permute-start | bytes 602120 | tf_op jit(solution)/shard_map/ppermute | solution.py:474

commit v3 on v2

--- a/solution.py
+++ b/solution.py
@@ -214,11 +214,10 @@
 
 
 def transform_kernel(
-    length, x_ref, forward_ref, backward_ref, w_hbm, out_ref, lat_ref, mix_ref, turn_ref, w_ref, sem
+    length, x_ref, forward_ref, backward_ref, w_hbm, out_ref, lat_ref, mix_ref, w_ref, sem
 ):
     f32, bf16 = jnp.float32, jnp.bfloat16
     rows = forward_ref.shape[0]
-    momenta = rows // 2
     tiles = x_ref.shape[1]
     spans = -(-length // LANES)
     copy = pltpu.make_async_copy(w_hbm, w_ref, sem)
@@ -278,12 +277,8 @@
         mixed = jnp.concatenate([mix_ref[j] for j in places], axis=1)
         projected = jnp.dot(backward_ref[...], mixed, preferred_element_type=f32).astype(bf16)
         for place, j in enumerate(places):
-            turn_ref[place] = x_tile(j)
-            for p in range(2):
-                half = slice(p * momenta, (p + 1) * momenta)
-                part = projected[half, place * LANES : (place + 1) * LANES].astype(f32)
-                own = turn_ref[place, pl.ds(p, momenta, stride=2), :]
-                out_ref[j, p] = (own + part).astype(bf16)
+            part = projected[:, place * LANES : (place + 1) * LANES].astype(f32)
+            out_ref[j] = (x_tile(j) + part).astype(bf16)
 
     by_pairs(backward)
 
@@ -295,15 +290,14 @@
         functools.partial(transform_kernel, length),
         in_specs=[whole(), whole(), whole(), pl.BlockSpec(memory_space=pl.ANY)],
         out_specs=whole(),
-        out_shape=jax.ShapeDtypeStruct((tiles, 2, rows // 2, LANES), jnp.bfloat16),
+        out_shape=jax.ShapeDtypeStruct((tiles, rows, LANES), jnp.bfloat16),
         scratch_shapes=[
             pltpu.VMEM((tiles, rows, LANES), jnp.bfloat16),
             pltpu.VMEM((tiles, rows, LANES), jnp.bfloat16),
-            pltpu.VMEM((2, rows, LANES), jnp.float32),
             pltpu.VMEM(w.shape, jnp.float32),
             pltpu.SemaphoreType.DMA,
         ],
-        compiler_params=pltpu.CompilerParams(vmem_limit_bytes=40 * 1024 * 1024),
+        compiler_params=pltpu.CompilerParams(vmem_limit_bytes=28 * 1024 * 1024),
     )(x, forward, backward, pltpu.with_memory_space_constraint(w, pltpu.HBM))
 
 
@@ -441,7 +435,7 @@
 
     forward, backward = phase_tables(momenta, MX, mesh_y, mesh_z)
     forward = forward.transpose(2, 3, 1, 0).reshape(2 * momenta, 2 * momenta)
-    backward = backward.transpose(2, 3, 0, 1).reshape(2 * momenta, 2 * momenta)
+    backward = backward.transpose(3, 2, 0, 1).reshape(2 * momenta, 2 * momenta)
     bond = jnp.arange(NB, dtype=jnp.int32)
     own = (jnp.arange(narrow, dtype=jnp.int32) * groups + lax.axis_index("pb")) % NB
     column_bonds = jnp.sum(
@@ -460,8 +454,10 @@
         axis=1,
     )
 
+    gathered, loops = lax.optimization_barrier((gathered, loops))
     united = transform(gathered, forward, backward, w, narrow * row_count)
-    united = united.transpose(2, 0, 1, 3)
+    tiles = united.shape[0]
+    united = united.reshape(tiles, momenta, 2, LANES).transpose(1, 0, 2, 3)
     sent = lax.all_to_all(united, ("pb", "col"), split_axis=0, concat_axis=0, tiled=True)
     u = sent.transpose(1, 2, 0, 3)
     mine = lax.axis_index("col").astype(jnp.int32).reshape(1)

time: 227 us -> 224 us (0.987)
  waiting for transfers between devices: 96.4 us -> 109 us
  local copies, waits for them, and re-layouts: 41.3 us -> 30 us
  other arithmetic: 11.8 us -> 8.52 us
    all_to_all x1, waiting for transfers between devices: 42.2 us -> 62.3 us  [per_device(): lax.all_to_all(united, ('pb', 'col'), split_axis=0, concat_axis=0, tiled=...]
    add x11, local copies, waits for them, and re-layouts: 10.4 us -> 0.2 us  [shifted_slots(): coords[axis][None, :] + sign * bond_offsets[:, axis][:, None]]
    all_to_all x1, waiting for transfers between devices: 23.6 us -> 16.1 us  [per_device(): lax.all_to_all(sent, 'pb', split_axis=0, concat_axis=0, tiled=True)]
    reshape x2, local copies, waits for them, and re-layouts: 8.65 us -> 11.2 us  [per_device(): loops = loop_blocks.reshape(3, order, 2, cols, row_count)]
  transfers between devices with their start and end apart: 11 -> 11, of which waited for: 6 -> 6; matrix products, arithmetic and copies ran while one was open for 20% -> 15% of each run, Pallas kernels for 7% -> 7%
where the time goes in v3:
time: 224 us; the launch traced here: 223 us
  waiting for transfers between devices  109 us (49%)
  starting transfers between devices  42.3 us (19%)
  Pallas kernels  32.1 us (14%)
  local copies, waits for them, and re-layouts  30 us (13%)
  other arithmetic  8.52 us (4%)
    all_to_all x1, waiting for transfers between devices, per_device(): lax.all_to_all(united, ('pb', 'col'), split_axis=0, concat_axis=0, tiled=...  62.3 us
    ppermute x9, waiting for transfers between devices, per_device(): lax.ppermute(pieces[k], 'col', [(i, i ^ k) for i in range(cols)])  30.3 us
    ppermute x9, starting transfers between devices, per_device(): lax.ppermute(pieces[k], 'col', [(i, i ^ k) for i in range(cols)])  19.8 us
    all_to_all x1, waiting for transfers between devices, per_device(): lax.all_to_all(sent, 'pb', split_axis=0, concat_axis=0, tiled=True)  16.1 us
    all_to_all x1, starting transfers between devices, per_device(): lax.all_to_all(sent, 'pb', split_axis=0, concat_axis=0, tiled=True)  12.7 us
    pallas_call x3, Pallas kernels, products(): pl.pallas_call(functools.partial(products_kernel, t), in_specs=[pl.BlockS...  11.7 us
    reshape x2, local copies, waits for them, and re-layouts, per_device(): loops = loop_blocks.reshape(3, order, 2, cols, row_count)  11.2 us
    all_to_all x1, starting transfers between devices, per_device(): lax.all_to_all(united, ('pb', 'col'), split_axis=0, concat_axis=0, tiled=...  9.69 us
  transfers between devices with their start and end apart: 11, of which 6 were waited for; matrix products, arithmetic and copies ran while one was open for 15% of the time, Pallas kernels for 7%

profile of v3, /device:TPU:1, one launch (start us, length us, event | category | flops | bytes accessed | tf_op | source)
XLA Modules:
  0.0 223.3 jit_solution(15716817298238485288)
XLA Ops:
  0.0 4.6 %shard_map.46 = bf16[64,19,8,128]{3,2,1,0:T(8,128)(2,1)} custom-call(bf16[3,4,112,896]{3,2,1,0:T(8,128)(2,1)} %v_ref.5), custom_call_target="tpu_custom_call" | custom-call | tf_op jit(solution)/shard_map/pallas_call | solution.py:200
  4.6 0.0 copy-start.4
  4.6 0.0 copy-start.3
  4.6 12.7 %all-to-all-start = ((bf16[64,19,8,128]{3,2,1,0:T(8,128)(2,1)}), bf16[64,19,8,128]{3,2,1,0:T(8,128)(2,1)S(1)}, u32[]{:S(2)}, u32[]{:S(2)}) async-start(bf16[64,19,8,128]{3,2,1,0:T(8,128)(2,1)} %shard_map.46), calls=%async_computation | async-start | bytes 4980736 | tf_op jit(solution)/shard_map/all_to_all | solution.py:434
  17.4 0.1 broadcast_reduce_fusion.2
  17.6 0.1 broadcast_reduce_fusion
  17.7 0.4 fusion.1
  18.2 0.6 reshape.779
  18.8 2.1 fusion.36
  21.0 0.1 maximum_bitcast_fusion.2
  21.0 0.5 copy.35
  21.5 0.1 copy.44
  21.6 1.3 maximum_bitcast_fusion
  22.9 0.1 fusion.5
  23.0 0.5 copy.34
  23.5 0.9 copy.43
  24.4 1.3 copy.39.forward_ref
  25.7 8.5 %reshape.775 = bf16[3,448,2,4,112]{4,3,2,1,0:T(4,128)(2,1)} reshape(bf16[3,1,448,896]{3,2,1,0:T(8,128)(2,1)} %param.5) | data formatting | bytes 4816896 | tf_op jit(solution)/shard_map/reshape | solution.py:446
  34.2 2.7 %copy.33 = bf16[3,448,2,4,112]{4,3,1,0,2:T(4,128)(2,1)S(1)} copy(bf16[3,448,2,4,112]{4,3,2,1,0:T(4,128)(2,1)} %reshape.775) | data formatting | bytes 4816896 | tf_op jit(solution)/shard_map/reshape | solution.py:446
  36.9 3.0 %pad.4 = bf16[3,448,2,4,128]{4,3,1,0,2:T(4,128)(2,1)} pad(bf16[3,448,2,4,112]{4,3,1,0,2:T(4,128)(2,1)S(1)} %copy.33, bf16[]{:T(256)} %constant.178.clone.1), padding=0_0x0_0x0_0x0_0x0_16 | pad | bytes 5160962 | tf_op jit(solution)/shard_map/jit(_pad)/pad | solution.py:447
  39.9 5.6 %reshape.776 = bf16[3,448,2,512]{3,1,0,2:T(8,128)(2,1)} reshape(bf16[3,448,2,4,128]{4,3,1,0,2:T(4,128)(2,1)} %pad.4) | data formatting | bytes 5505024 | tf_op jit(solution)/shard_map/reshape | solution.py:447
  45.6 0.1 iota_compare_fusion.3
  45.6 0.1 select_reduce_fusion
  45.8 0.1 fusion.48
  45.9 0.8 reduce-precision_convert_fusion.3
  46.7 0.3 fusion.picks_ref
  47.0 0.5 fusion.14
  47.5 0.1 reduce-precision_convert_fusion.1
  47.7 0.1 reduce-precision_convert_fusion
  47.8 0.1 pad_maximum_fusion.wide_ref
  47.9 6.2 %shard_map.47.w_hbm = f32[6,256,896]{2,1,0:T(8,128)S(1)} custom-call(bf16[7,256,256]{2,1,0:T(8,128)(2,1)S(1)} %fusion.picks_ref, bf16[256,2304]{1,0:T(8,128)(2,1)S(1)} %pad_maximum_fusion.wide_ref), custom_call_target="tpu_custom_call" | custom-call | tf_op jit(solution)/shard_map/pallas_call | solution.py:83
  54.2 0.1 fusion.73
  54.3 0.2 slice_bitcast_fusion
  54.4 2.2 copy-done.1
  56.6 3.0 %maximum_maximum_fusion.loop_hbm = bf16[3,896,1024]{2,1,0:T(8,128)(2,1)} fusion(bf16[3,448,512]{2,1,0:T(8,128)(2,1)S(1)} %get-tuple-element.42, bf16[3,448,512]{2,1,0:T(8,128)(2,1)S(1)} %fusion.73, bf16[3,448,512]{2,1,0:T(8,128)(2,1)S(1)} %get-tuple-element.41), kind=kLoop, calls=%fused_computation | loop fusion | flops 22020096 | bytes 9633792 | tf_op jit(solution)/shard_map/concatenate | solution.py:449
  59.6 16.1 %all-to-all-done.x_ref = bf16[64,19,8,128]{3,2,1,0:T(8,128)(2,1)S(1)} async-done(((bf16[64,19,8,128]{3,2,1,0:T(8,128)(2,1)}), bf16[64,19,8,128]{3,2,1,0:T(8,128)(2,1)S(1)}, u32[]{:S(2)}, u32[]{:S(2)}) %all-to-all-start) | async-done | bytes 2490400 | tf_op jit(solution)/shard_map/all_to_all | solution.py:434
  75.7 6.7 %shard_map.48 = bf16[19,512,128]{2,1,0:T(8,128)(2,1)S(1)} custom-call(bf16[64,19,8,128]{3,2,1,0:T(8,128)(2,1)S(1)} %all-to-all-done.x_ref, bf16[512,512]{1,0:T(8,128)(2,1)S(1)} %copy.39.forward_ref, bf16[512,512]{1,0:T(8,128)(2,1)S(1)} %bitcast.60, f32[6,256,896]{2,1,0:T(8,128)} %copy-done.1), custom_call_target="tpu_custom_call" | custom-call | tf_op jit(solution)/shard_map/pallas_call | solution.py:289
  82.5 3.2 %copy.40 = bf16[256,19,2,128]{3,2,1,0:T(2,128)(2,1)} copy(bf16[256,19,2,128]{3,2,0,1:T(2,128)(2,1)S(1)} %bitcast.59) | data formatting | bytes 4980736 | tf_op jit(solution)/shard_map/transpose | solution.py:460
  85.6 9.7 %all-to-all-start.1 = ((bf16[256,19,2,128]{3,2,1,0:T(2,128)(2,1)}), bf16[256,19,2,128]{3,2,1,0:T(2,128)(2,1)S(1)}, u32[]{:S(2)}, u32[]{:S(2)}) async-start(bf16[256,19,2,128]{3,2,1,0:T(2,128)(2,1)} %copy.40), calls=%async_computation.1 | async-start | bytes 4980736 | tf_op jit(solution)/shard_map/all_to_all | solution.py:461
  95.3 62.3 %all-to-all-done.1 = bf16[256,19,2,128]{3,2,1,0:T(2,128)(2,1)S(1)} async-done(((bf16[256,19,2,128]{3,2,1,0:T(2,128)(2,1)}), bf16[256,19,2,128]{3,2,1,0:T(2,128)(2,1)S(1)}, u32[]{:S(2)}, u32[]{:S(2)}) %all-to-all-start.1) | async-done | bytes 2490400 | tf_op jit(solution)/shard_map/all_to_all | solution.py:461
  157.7 0.6 copy.46
  158.2 3.9 %shard_map.49 = (bf16[112,896]{1,0:T(8,128)(2,1)S(1)}, bf16[112,896]{1,0:T(8,128)(2,1)S(1)}, bf16[112,896]{1,0:T(8,128)(2,1)S(1)}, bf16[112,896]{1,0:T(8,128)(2,1)S(1)}) custom-call(s32[1]{0:T(128)} %bitcast.mine_ref, bf16[19,2,256,128]{3,2,1,0:T(8,128)(2,1)S(1)} %bitcast.56, bf16[3,896,1024]{2,1,0:T(8,128)(2,1)} %maximum_maximum_fusion.loop_hbm), custom_call_target="tpu_custom_call" | custom-call | tf_op jit(solution)/shard_map/pallas_call | solution.py:364
  162.1 1.8 collective-permute-start
  163.9 0.5 collective-permute-start.7
  164.4 5.1 %collective-permute-start.8 = (bf16[112,896]{1,0:T(8,128)(2,1)S(1)}, bf16[112,896]{1,0:T(8,128)(2,1)S(1)}, u32[]{:S(2)}, u32[]{:S(2)}) collective-permute-start(bf16[112,896]{1,0:T(8,128)(2,1)S(1)} %get-tuple-element.38), channel_id=1, source_target_pairs={{0,3},{1,2},{2,1},{3,0},{4,7},{5,6},{6,5},{7,4},{8,11},{9,10},{10,... | collective-permute-start | bytes 602120 | tf_op jit(solution)/shard_map/ppermute | solution.py:470
  169.6 0.0 collective-permute-done.refs_1_
  169.6 3.9 %shard_map.51 = (bf16[112,896]{1,0:T(8,128)(2,1)S(1)}, bf16[112,896]{1,0:T(8,128)(2,1)S(1)}, bf16[112,896]{1,0:T(8,128)(2,1)S(1)}, bf16[112,896]{1,0:T(8,128)(2,1)S(1)}) custom-call(s32[1]{0:T(128)} %bitcast.mine_ref, bf16[19,2,256,128]{3,2,1,0:T(8,128)(2,1)S(1)} %bitcast.57, bf16[3,896,1024]{2,1,0:T(8,128)(2,1)} %maximum_maximum_fusion.loop_hbm), custom_call_target="tpu_custom_call" | custom-call | tf_op jit(solution)/shard_map/pallas_call | solution.py:364
  173.4 0.0 copy-start
  173.5 0.2 collective-permute-start.4
  173.7 4.0 %shard_map.50 = (bf16[112,896]{1,0:T(8,128)(2,1)S(1)}, bf16[112,896]{1,0:T(8,128)(2,1)S(1)}, bf16[112,896]{1,0:T(8,128)(2,1)S(1)}, bf16[112,896]{1,0:T(8,128)(2,1)S(1)}) custom-call(s32[1]{0:T(128)} %bitcast.mine_ref, bf16[19,2,256,128]{3,2,1,0:T(8,128)(2,1)S(1)} %bitcast.58, bf16[3,896,1024]{2,1,0:T(8,128)(2,1)} %maximum_maximum_fusion.loop_hbm), custom_call_target="tpu_custom_call" | custom-call | tf_op jit(solution)/shard_map/pallas_call | solution.py:364
  177.7 0.6 collective-permute-start.5
  178.3 5.5 %collective-permute-start.6 = (bf16[112,896]{1,0:T(8,128)(2,1)S(1)}, bf16[112,896]{1,0:T(8,128)(2,1)S(1)}, u32[]{:S(2)}, u32[]{:S(2)}) collective-permute-start(bf16[112,896]{1,0:T(8,128)(2,1)S(1)} %get-tuple-element.34), channel_id=1, source_target_pairs={{0,3},{1,2},{2,1},{3,0},{4,7},{5,6},{6,5},{7,4},{8,11},{9,10},{10,... | collective-permute-start | bytes 602120 | tf_op jit(solution)/shard_map/ppermute | solution.py:470
  183.8 0.0 collective-permute-done.7.refs_2_
  183.8 0.0 collective-permute-start.1
  183.8 0.6 collective-permute-start.2
  184.4 5.5 %collective-permute-start.3 = (bf16[112,896]{1,0:T(8,128)(2,1)S(1)}, bf16[112,896]{1,0:T(8,128)(2,1)S(1)}, u32[]{:S(2)}, u32[]{:S(2)}) collective-permute-start(bf16[112,896]{1,0:T(8,128)(2,1)S(1)} %get-tuple-element.29), channel_id=1, source_target_pairs={{0,3},{1,2},{2,1},{3,0},{4,7},{5,6},{6,5},{7,4},{8,11},{9,10},{10,... | collective-permute-start | bytes 602120 | tf_op jit(solution)/shard_map/ppermute | solution.py:470
  189.9 1.0 shard_map.52.refs_4_
  190.8 6.8 %collective-permute-done.5.refs_2_ = bf16[112,896]{1,0:T(8,128)(2,1)S(1)} collective-permute-done((bf16[112,896]{1,0:T(8,128)(2,1)S(1)}, bf16[112,896]{1,0:T(8,128)(2,1)S(1)}, u32[]{:S(2)}, u32[]{:S(2)}) %collective-permute-start.5) | collective-permute-done | bytes 200736 | tf_op jit(solution)/shard_map/ppermute | solution.py:470
  197.6 11.4 %collective-permute-done.6.refs_3_ = bf16[112,896]{1,0:T(8,128)(2,1)S(1)} collective-permute-done((bf16[112,896]{1,0:T(8,128)(2,1)S(1)}, bf16[112,896]{1,0:T(8,128)(2,1)S(1)}, u32[]{:S(2)}, u32[]{:S(2)}) %collective-permute-start.6) | collective-permute-done | bytes 200736 | tf_op jit(solution)/shard_map/ppermute | solution.py:470
  209.0 1.0 shard_map.53.refs_4_
  210.0 0.0 collective-permute-done.1.refs_1_
  210.0 7.8 %collective-permute-done.2.refs_2_ = bf16[112,896]{1,0:T(8,128)(2,1)S(1)} collective-permute-done((bf16[112,896]{1,0:T(8,128)(2,1)S(1)}, bf16[112,896]{1,0:T(8,128)(2,1)S(1)}, u32[]{:S(2)}, u32[]{:S(2)}) %collective-permute-start.2) | collective-permute-done | bytes 200736 | tf_op jit(solution)/shard_map/ppermute | solution.py:470
  217.8 4.3 %collective-permute-done.3.refs_3_ = bf16[112,896]{1,0:T(8,128)(2,1)S(1)} collective-permute-done((bf16[112,896]{1,0:T(8,128)(2,1)S(1)}, bf16[112,896]{1,0:T(8,128)(2,1)S(1)}, u32[]{:S(2)}, u32[]{:S(2)}) %collective-permute-start.3) | collective-permute-done | bytes 200736 | tf_op jit(solution)/shard_map/ppermute | solution.py:470
  222.1 1.0 shard_map.54
  (29 shorter events, 0.2 us)
Async XLA Ops:
  4.6 12.8 %copy-start.4 = (s32[7,3]{0,1:T(4,128)S(1)}, s32[7,3]{0,1:T(4,128)}, u32[]{:S(2)}) copy-start(s32[7,3]{0,1:T(4,128)} %param.7) | copy-start | bytes 256
  4.6 13.0 %copy-start.3 = (f32[6,256]{1,0:T(8,128)S(1)}, f32[6,256]{1,0:T(8,128)}, u32[]{:S(2)}) copy-start(f32[6,256]{1,0:T(8,128)} %param.6) | copy-start | bytes 18436
  4.6 71.1 %all-to-all-start = ((bf16[64,19,8,128]{3,2,1,0:T(8,128)(2,1)}), bf16[64,19,8,128]{3,2,1,0:T(8,128)(2,1)S(1)}, u32[]{:S(2)}, u32[]{:S(2)}) async-start(bf16[64,19,8,128]{3,2,1,0:T(8,128)(2,1)} %shard_map.46), calls=%async_computation | async-start | bytes 4980736 | tf_op jit(solution)/shard_map/all_to_all | solution.py:434
  47.9 6.3 %copy-start.2 = (bf16[3,448,2,512]{3,1,0,2:T(8,128)(2,1)S(1)}, bf16[3,448,2,512]{3,1,0,2:T(8,128)(2,1)}, u32[]{:S(2)}) copy-start(bf16[3,448,2,512]{3,1,0,2:T(8,128)(2,1)} %reshape.776) | copy-start | bytes 8257540
  54.1 2.5 %copy-start.1 = (f32[6,256,896]{2,1,0:T(8,128)}, f32[6,256,896]{2,1,0:T(8,128)S(1)}, u32[]{:S(2)}) copy-start(f32[6,256,896]{2,1,0:T(8,128)S(1)} %shard_map.47.w_hbm) | copy-start | bytes 16515076
  85.6 72.0 %all-to-all-start.1 = ((bf16[256,19,2,128]{3,2,1,0:T(2,128)(2,1)}), bf16[256,19,2,128]{3,2,1,0:T(2,128)(2,1)S(1)}, u32[]{:S(2)}, u32[]{:S(2)}) async-start(bf16[256,19,2,128]{3,2,1,0:T(2,128)(2,1)} %copy.40), calls=%async_computation.1 | async-start | bytes 4980736 | tf_op jit(solution)/shard_map/all_to_all | solution.py:461
  162.1 7.5 %collective-permute-start = (bf16[112,896]{1,0:T(8,128)(2,1)S(1)}, bf16[112,896]{1,0:T(8,128)(2,1)S(1)}, u32[]{:S(2)}, u32[]{:S(2)}) collective-permute-start(bf16[112,896]{1,0:T(8,128)(2,1)S(1)} %get-tuple-element.24), channel_id=1, source_target_pairs={{0,1},{1,0},{2,3},{3,2},{4,5},{5,4},{6,7},{7,6},{8,9},{9,8},{10,11... | collective-permute-start | bytes 602120 | tf_op jit(solution)/shard_map/ppermute | solution.py:470
  163.9 19.9 %collective-permute-start.7 = (bf16[112,896]{1,0:T(8,128)(2,1)S(1)}, bf16[112,896]{1,0:T(8,128)(2,1)S(1)}, u32[]{:S(2)}, u32[]{:S(2)}) collective-permute-start(bf16[112,896]{1,0:T(8,128)(2,1)S(1)} %get-tuple-element.37), channel_id=1, source_target_pairs={{0,2},{1,3},{2,0},{3,1},{4,6},{5,7},{6,4},{7,5},{8,10},{9,11},{10,... | collective-permute-start | bytes 602120 | tf_op jit(solution)/shard_map/ppermute | solution.py:470
  164.4 19.4 %collective-permute-start.8 = (bf16[112,896]{1,0:T(8,128)(2,1)S(1)}, bf16[112,896]{1,0:T(8,128)(2,1)S(1)}, u32[]{:S(2)}, u32[]{:S(2)}) collective-permute-start(bf16[112,896]{1,0:T(8,128)(2,1)S(1)} %get-tuple-element.38), channel_id=1, source_target_pairs={{0,3},{1,2},{2,1},{3,0},{4,7},{5,6},{6,5},{7,4},{8,11},{9,10},{10,... | collective-permute-start | bytes 602120 | tf_op jit(solution)/shard_map/ppermute | solution.py:470
  173.4 16.4 %copy-start = (bf16[3,4,112,896]{3,2,1,0:T(8,128)(2,1)S(1)}, bf16[3,4,112,896]{3,2,1,0:T(8,128)(2,1)}, u32[]{:S(2)}) copy-start(bf16[3,4,112,896]{3,2,1,0:T(8,128)(2,1)} %v_ref.5) | copy-start | bytes 7225348
  173.5 10.9 %collective-permute-start.4 = (bf16[112,896]{1,0:T(8,128)(2,1)S(1)}, bf16[112,896]{1,0:T(8,128)(2,1)S(1)}, u32[]{:S(2)}, u32[]{:S(2)}) collective-permute-start(bf16[112,896]{1,0:T(8,128)(2,1)S(1)} %get-tuple-element.32), channel_id=1, source_target_pairs={{0,1},{1,0},{2,3},{3,2},{4,5},{5,4},{6,7},{7,6},{8,9},{9,8},{10,11... | collective-permute-start | bytes 602120 | tf_op jit(solution)/shard_map/ppermute | solution.py:470
  177.7 19.9 %collective-permute-start.5 = (bf16[112,896]{1,0:T(8,128)(2,1)S(1)}, bf16[112,896]{1,0:T(8,128)(2,1)S(1)}, u32[]{:S(2)}, u32[]{:S(2)}) collective-permute-start(bf16[112,896]{1,0:T(8,128)(2,1)S(1)} %get-tuple-element.33), channel_id=1, source_target_pairs={{0,2},{1,3},{2,0},{3,1},{4,6},{5,7},{6,4},{7,5},{8,10},{9,11},{10,... | collective-permute-start | bytes 602120 | tf_op jit(solution)/shard_map/ppermute | solution.py:470
  178.3 30.7 %collective-permute-start.6 = (bf16[112,896]{1,0:T(8,128)(2,1)S(1)}, bf16[112,896]{1,0:T(8,128)(2,1)S(1)}, u32[]{:S(2)}, u32[]{:S(2)}) collective-permute-start(bf16[112,896]{1,0:T(8,128)(2,1)S(1)} %get-tuple-element.34), channel_id=1, source_target_pairs={{0,3},{1,2},{2,1},{3,0},{4,7},{5,6},{6,5},{7,4},{8,11},{9,10},{10,... | collective-permute-start | bytes 602120 | tf_op jit(solution)/shard_map/ppermute | solution.py:470
  183.8 26.2 %collective-permute-start.1 = (bf16[112,896]{1,0:T(8,128)(2,1)S(1)}, bf16[112,896]{1,0:T(8,128)(2,1)S(1)}, u32[]{:S(2)}, u32[]{:S(2)}) collective-permute-start(bf16[112,896]{1,0:T(8,128)(2,1)S(1)} %get-tuple-element.27), channel_id=1, source_target_pairs={{0,1},{1,0},{2,3},{3,2},{4,5},{5,4},{6,7},{7,6},{8,9},{9,8},{10,11... | collective-permute-start | bytes 602120 | tf_op jit(solution)/shard_map/ppermute | solution.py:470
  183.8 34.0 %collective-permute-start.2 = (bf16[112,896]{1,0:T(8,128)(2,1)S(1)}, bf16[112,896]{1,0:T(8,128)(2,1)S(1)}, u32[]{:S(2)}, u32[]{:S(2)}) collective-permute-start(bf16[112,896]{1,0:T(8,128)(2,1)S(1)} %get-tuple-element.28), channel_id=1, source_target_pairs={{0,2},{1,3},{2,0},{3,1},{4,6},{5,7},{6,4},{7,5},{8,10},{9,11},{10,... | collective-permute-start | bytes 602120 | tf_op jit(solution)/shard_map/ppermute | solution.py:470
  184.4 37.7 %collective-permute-start.3 = (bf16[112,896]{1,0:T(8,128)(2,1)S(1)}, bf16[112,896]{1,0:T(8,128)(2,1)S(1)}, u32[]{:S(2)}, u32[]{:S(2)}) collective-permute-start(bf16[112,896]{1,0:T(8,128)(2,1)S(1)} %get-tuple-element.29), channel_id=1, source_target_pairs={{0,3},{1,2},{2,1},{3,0},{4,7},{5,6},{6,5},{7,4},{8,11},{9,10},{10,... | collective-permute-start | bytes 602120 | tf_op jit(solution)/shard_map/ppermute | solution.py:470

commit v4 on v3

--- a/solution.py
+++ b/solution.py
@@ -214,7 +214,7 @@
 
 
 def transform_kernel(
-    length, x_ref, forward_ref, backward_ref, w_hbm, out_ref, lat_ref, mix_ref, w_ref, sem
+    length, x_ref, forward_ref, backward_ref, w_hbm, out_hbm, lat_ref, mix_ref, out_ref, w_ref, sem, out_sems
 ):
     f32, bf16 = jnp.float32, jnp.bfloat16
     rows = forward_ref.shape[0]
@@ -278,9 +278,16 @@
         projected = jnp.dot(backward_ref[...], mixed, preferred_element_type=f32).astype(bf16)
         for place, j in enumerate(places):
             part = projected[:, place * LANES : (place + 1) * LANES].astype(f32)
-            out_ref[j] = (x_tile(j) + part).astype(bf16)
+            united = (x_tile(j) + part).astype(bf16)
+            out_ref[j] = united.reshape(rows // 2, 2, LANES)
+            leaving(j).start()
+
+    def leaving(j):
+        return pltpu.make_async_copy(out_ref.at[j], out_hbm.at[:, j], out_sems.at[j])
 
     by_pairs(backward)
+    for j in range(tiles):
+        leaving(j).wait()
 
 
 def transform(x, forward, backward, w, length):
@@ -289,13 +296,15 @@
     return pl.pallas_call(
         functools.partial(transform_kernel, length),
         in_specs=[whole(), whole(), whole(), pl.BlockSpec(memory_space=pl.ANY)],
-        out_specs=whole(),
-        out_shape=jax.ShapeDtypeStruct((tiles, rows, LANES), jnp.bfloat16),
+        out_specs=pl.BlockSpec(memory_space=pltpu.HBM),
+        out_shape=pltpu.HBM((rows // 2, tiles, 2, LANES), jnp.bfloat16),
         scratch_shapes=[
             pltpu.VMEM((tiles, rows, LANES), jnp.bfloat16),
             pltpu.VMEM((tiles, rows, LANES), jnp.bfloat16),
+            pltpu.VMEM((tiles, rows // 2, 2, LANES), jnp.bfloat16),
             pltpu.VMEM(w.shape, jnp.float32),
             pltpu.SemaphoreType.DMA,
+            pltpu.SemaphoreType.DMA((tiles,)),
         ],
         compiler_params=pltpu.CompilerParams(vmem_limit_bytes=28 * 1024 * 1024),
     )(x, forward, backward, pltpu.with_memory_space_constraint(w, pltpu.HBM))
@@ -456,8 +465,6 @@
 
     gathered, loops = lax.optimization_barrier((gathered, loops))
     united = transform(gathered, forward, backward, w, narrow * row_count)
-    tiles = united.shape[0]
-    united = united.reshape(tiles, momenta, 2, LANES).transpose(1, 0, 2, 3)
     sent = lax.all_to_all(united, ("pb", "col"), split_axis=0, concat_axis=0, tiled=True)
     u = sent.transpose(1, 2, 0, 3)
     mine = lax.axis_index("col").astype(jnp.int32).reshape(1)

time: 224 us -> 223 us (level)
  local copies, waits for them, and re-layouts: 30 us -> 26.9 us
  Pallas kernels: 32.1 us -> 34.7 us
    transpose x1 -> x0, local copies, waits for them, and re-layouts: 3.17 us -> none  [per_device(): united = united.reshape(tiles, momenta, 2, LANES).transpose(1, 0, 2, 3)]
    pallas_call x1, Pallas kernels: 6.72 us -> 9.3 us  [transform(): pl.pallas_call(functools.partial(transform_kernel, length), in_specs=[who...]
where the time goes in v4:
time: 223 us
  waiting for transfers between devices  109 us (49%)
  starting transfers between devices  42.3 us (19%)
  Pallas kernels  34.7 us (16%)
  local copies, waits for them, and re-layouts  26.9 us (12%)
  other arithmetic  8.52 us (4%)
    all_to_all x1, waiting for transfers between devices, per_device(): lax.all_to_all(united, ('pb', 'col'), split_axis=0, concat_axis=0, tiled=...  62.3 us
    ppermute x9, waiting for transfers between devices, per_device(): lax.ppermute(pieces[k], 'col', [(i, i ^ k) for i in range(cols)])  30.3 us
    ppermute x9, starting transfers between devices, per_device(): lax.ppermute(pieces[k], 'col', [(i, i ^ k) for i in range(cols)])  19.8 us
    all_to_all x1, waiting for transfers between devices, per_device(): lax.all_to_all(sent, 'pb', split_axis=0, concat_axis=0, tiled=True)  16.1 us
    all_to_all x1, starting transfers between devices, per_device(): lax.all_to_all(sent, 'pb', split_axis=0, concat_axis=0, tiled=True)  12.7 us
    pallas_call x3, Pallas kernels, products(): pl.pallas_call(functools.partial(products_kernel, t), in_specs=[pl.BlockS...  11.8 us
    reshape x2, local copies, waits for them, and re-layouts, per_device(): loops = loop_blocks.reshape(3, order, 2, cols, row_count)  11.2 us
    all_to_all x1, starting transfers between devices, per_device(): lax.all_to_all(united, ('pb', 'col'), split_axis=0, concat_axis=0, tiled=...  9.7 us
  transfers between devices with their start and end apart: 11, of which 6 were waited for; matrix products, arithmetic and copies ran while one was open for 15% of the time, Pallas kernels for 7%

profile of v4, /device:TPU:1, one launch (start us, length us, event | category | flops | bytes accessed | tf_op | source)
XLA Modules:
  0.0 222.7 jit_solution(10943602509365504826)
XLA Ops:
  0.0 4.6 %shard_map.46 = bf16[64,19,8,128]{3,2,1,0:T(8,128)(2,1)} custom-call(bf16[3,4,112,896]{3,2,1,0:T(8,128)(2,1)} %v_ref.5), custom_call_target="tpu_custom_call" | custom-call | tf_op jit(solution)/shard_map/pallas_call | solution.py:200
  4.6 0.0 copy-start.4
  4.6 0.0 copy-start.3
  4.6 12.7 %all-to-all-start = ((bf16[64,19,8,128]{3,2,1,0:T(8,128)(2,1)}), bf16[64,19,8,128]{3,2,1,0:T(8,128)(2,1)S(1)}, u32[]{:S(2)}, u32[]{:S(2)}) async-start(bf16[64,19,8,128]{3,2,1,0:T(8,128)(2,1)} %shard_map.46), calls=%async_computation | async-start | bytes 4980736 | tf_op jit(solution)/shard_map/all_to_all | solution.py:443
  17.4 0.1 broadcast_reduce_fusion.2
  17.6 0.1 broadcast_reduce_fusion
  17.7 0.4 fusion.1
  18.2 0.6 reshape.776
  18.8 2.1 fusion.36
  21.0 0.1 maximum_bitcast_fusion.2
  21.0 0.5 copy.35
  21.5 0.1 copy.43
  21.6 1.3 maximum_bitcast_fusion
  22.9 0.1 fusion.5
  23.0 0.5 copy.34
  23.5 0.9 copy.42
  24.4 1.3 copy.39.forward_ref
  25.7 8.5 %reshape.772 = bf16[3,448,2,4,112]{4,3,2,1,0:T(4,128)(2,1)} reshape(bf16[3,1,448,896]{3,2,1,0:T(8,128)(2,1)} %param.5) | data formatting | bytes 4816896 | tf_op jit(solution)/shard_map/reshape | solution.py:455
  34.2 2.7 %copy.33 = bf16[3,448,2,4,112]{4,3,1,0,2:T(4,128)(2,1)S(1)} copy(bf16[3,448,2,4,112]{4,3,2,1,0:T(4,128)(2,1)} %reshape.772) | data formatting | bytes 4816896 | tf_op jit(solution)/shard_map/reshape | solution.py:455
  36.9 3.0 %pad.4 = bf16[3,448,2,4,128]{4,3,1,0,2:T(4,128)(2,1)} pad(bf16[3,448,2,4,112]{4,3,1,0,2:T(4,128)(2,1)S(1)} %copy.33, bf16[]{:T(256)} %constant.178.clone.1), padding=0_0x0_0x0_0x0_0x0_16 | pad | bytes 5160962 | tf_op jit(solution)/shard_map/jit(_pad)/pad | solution.py:456
  39.9 5.6 %reshape.773 = bf16[3,448,2,512]{3,1,0,2:T(8,128)(2,1)} reshape(bf16[3,448,2,4,128]{4,3,1,0,2:T(4,128)(2,1)} %pad.4) | data formatting | bytes 5505024 | tf_op jit(solution)/shard_map/reshape | solution.py:456
  45.6 0.1 iota_compare_fusion.3
  45.6 0.1 select_reduce_fusion
  45.8 0.1 fusion.48
  45.9 0.8 reduce-precision_convert_fusion.3
  46.7 0.3 fusion.picks_ref
  47.0 0.5 fusion.14
  47.5 0.1 reduce-precision_convert_fusion.1
  47.7 0.1 reduce-precision_convert_fusion
  47.8 0.1 pad_maximum_fusion.wide_ref
  47.9 6.2 %shard_map.47.w_hbm = f32[6,256,896]{2,1,0:T(8,128)S(1)} custom-call(bf16[7,256,256]{2,1,0:T(8,128)(2,1)S(1)} %fusion.picks_ref, bf16[256,2304]{1,0:T(8,128)(2,1)S(1)} %pad_maximum_fusion.wide_ref), custom_call_target="tpu_custom_call" | custom-call | tf_op jit(solution)/shard_map/pallas_call | solution.py:83
  54.2 0.1 fusion.73
  54.3 0.2 slice_bitcast_fusion
  54.4 2.2 copy-done.1
  56.6 3.0 %maximum_maximum_fusion.loop_hbm = bf16[3,896,1024]{2,1,0:T(8,128)(2,1)} fusion(bf16[3,448,512]{2,1,0:T(8,128)(2,1)S(1)} %get-tuple-element.42, bf16[3,448,512]{2,1,0:T(8,128)(2,1)S(1)} %fusion.73, bf16[3,448,512]{2,1,0:T(8,128)(2,1)S(1)} %get-tuple-element.41), kind=kLoop, calls=%fused_computation | loop fusion | flops 22020096 | bytes 9633792 | tf_op jit(solution)/shard_map/concatenate | solution.py:458
  59.6 16.1 %all-to-all-done.x_ref = bf16[64,19,8,128]{3,2,1,0:T(8,128)(2,1)S(1)} async-done(((bf16[64,19,8,128]{3,2,1,0:T(8,128)(2,1)}), bf16[64,19,8,128]{3,2,1,0:T(8,128)(2,1)S(1)}, u32[]{:S(2)}, u32[]{:S(2)}) %all-to-all-start) | async-done | bytes 2490400 | tf_op jit(solution)/shard_map/all_to_all | solution.py:443
  75.7 9.3 %shard_map.48 = bf16[256,19,2,128]{3,2,1,0:T(2,128)(2,1)} custom-call(bf16[64,19,8,128]{3,2,1,0:T(8,128)(2,1)S(1)} %all-to-all-done.x_ref, bf16[512,512]{1,0:T(8,128)(2,1)S(1)} %copy.39.forward_ref, bf16[512,512]{1,0:T(8,128)(2,1)S(1)} %bitcast.56, f32[6,256,896]{2,1,0:T(8,128)} %copy-done.1), custom_call_target="tpu_custom_call" | custom-call | tf_op jit(solution)/shard_map/pallas_call | solution.py:296
  85.0 9.7 %all-to-all-start.1 = ((bf16[256,19,2,128]{3,2,1,0:T(2,128)(2,1)}), bf16[256,19,2,128]{3,2,1,0:T(2,128)(2,1)S(1)}, u32[]{:S(2)}, u32[]{:S(2)}) async-start(bf16[256,19,2,128]{3,2,1,0:T(2,128)(2,1)} %shard_map.48), calls=%async_computation.1 | async-start | bytes 4980736 | tf_op jit(solution)/shard_map/all_to_all | solution.py:468
  94.8 62.3 %all-to-all-done.1 = bf16[256,19,2,128]{3,2,1,0:T(2,128)(2,1)S(1)} async-done(((bf16[256,19,2,128]{3,2,1,0:T(2,128)(2,1)}), bf16[256,19,2,128]{3,2,1,0:T(2,128)(2,1)S(1)}, u32[]{:S(2)}, u32[]{:S(2)}) %all-to-all-start.1) | async-done | bytes 2490400 | tf_op jit(solution)/shard_map/all_to_all | solution.py:468
  157.1 0.6 copy.45
  157.6 3.9 %shard_map.49 = (bf16[112,896]{1,0:T(8,128)(2,1)S(1)}, bf16[112,896]{1,0:T(8,128)(2,1)S(1)}, bf16[112,896]{1,0:T(8,128)(2,1)S(1)}, bf16[112,896]{1,0:T(8,128)(2,1)S(1)}) custom-call(s32[1]{0:T(128)} %bitcast.mine_ref, bf16[19,2,256,128]{3,2,1,0:T(8,128)(2,1)S(1)} %bitcast.53, bf16[3,896,1024]{2,1,0:T(8,128)(2,1)} %maximum_maximum_fusion.loop_hbm), custom_call_target="tpu_custom_call" | custom-call | tf_op jit(solution)/shard_map/pallas_call | solution.py:373
  161.5 1.8 collective-permute-start
  163.3 0.5 collective-permute-start.7
  163.9 5.1 %collective-permute-start.8 = (bf16[112,896]{1,0:T(8,128)(2,1)S(1)}, bf16[112,896]{1,0:T(8,128)(2,1)S(1)}, u32[]{:S(2)}, u32[]{:S(2)}) collective-permute-start(bf16[112,896]{1,0:T(8,128)(2,1)S(1)} %get-tuple-element.38), channel_id=1, source_target_pairs={{0,3},{1,2},{2,1},{3,0},{4,7},{5,6},{6,5},{7,4},{8,11},{9,10},{10,... | collective-permute-start | bytes 602120 | tf_op jit(solution)/shard_map/ppermute | solution.py:477
  169.0 0.0 collective-permute-done.refs_1_
  169.0 3.9 %shard_map.51 = (bf16[112,896]{1,0:T(8,128)(2,1)S(1)}, bf16[112,896]{1,0:T(8,128)(2,1)S(1)}, bf16[112,896]{1,0:T(8,128)(2,1)S(1)}, bf16[112,896]{1,0:T(8,128)(2,1)S(1)}) custom-call(s32[1]{0:T(128)} %bitcast.mine_ref, bf16[19,2,256,128]{3,2,1,0:T(8,128)(2,1)S(1)} %bitcast.54, bf16[3,896,1024]{2,1,0:T(8,128)(2,1)} %maximum_maximum_fusion.loop_hbm), custom_call_target="tpu_custom_call" | custom-call | tf_op jit(solution)/shard_map/pallas_call | solution.py:373
  172.9 0.0 copy-start
  172.9 0.2 collective-permute-start.4
  173.1 4.0 %shard_map.50 = (bf16[112,896]{1,0:T(8,128)(2,1)S(1)}, bf16[112,896]{1,0:T(8,128)(2,1)S(1)}, bf16[112,896]{1,0:T(8,128)(2,1)S(1)}, bf16[112,896]{1,0:T(8,128)(2,1)S(1)}) custom-call(s32[1]{0:T(128)} %bitcast.mine_ref, bf16[19,2,256,128]{3,2,1,0:T(8,128)(2,1)S(1)} %bitcast.55, bf16[3,896,1024]{2,1,0:T(8,128)(2,1)} %maximum_maximum_fusion.loop_hbm), custom_call_target="tpu_custom_call" | custom-call | tf_op jit(solution)/shard_map/pallas_call | solution.py:373
  177.1 0.6 collective-permute-start.5
  177.7 5.5 %collective-permute-start.6 = (bf16[112,896]{1,0:T(8,128)(2,1)S(1)}, bf16[112,896]{1,0:T(8,128)(2,1)S(1)}, u32[]{:S(2)}, u32[]{:S(2)}) collective-permute-start(bf16[112,896]{1,0:T(8,128)(2,1)S(1)} %get-tuple-element.34), channel_id=1, source_target_pairs={{0,3},{1,2},{2,1},{3,0},{4,7},{5,6},{6,5},{7,4},{8,11},{9,10},{10,... | collective-permute-start | bytes 602120 | tf_op jit(solution)/shard_map/ppermute | solution.py:477
  183.2 0.0 collective-permute-done.7.refs_2_
  183.2 0.0 collective-permute-start.1
  183.2 0.0 collective-permute-done.8.refs_3_
  183.2 0.6 collective-permute-start.2
  183.8 0.0 collective-permute-done.4.refs_1_
  183.8 5.5 %collective-permute-start.3 = (bf16[112,896]{1,0:T(8,128)(2,1)S(1)}, bf16[112,896]{1,0:T(8,128)(2,1)S(1)}, u32[]{:S(2)}, u32[]{:S(2)}) collective-permute-start(bf16[112,896]{1,0:T(8,128)(2,1)S(1)} %get-tuple-element.29), channel_id=1, source_target_pairs={{0,3},{1,2},{2,1},{3,0},{4,7},{5,6},{6,5},{7,4},{8,11},{9,10},{10,... | collective-permute-start | bytes 602120 | tf_op jit(solution)/shard_map/ppermute | solution.py:477
  189.3 1.0 shard_map.52.refs_4_
  190.2 6.8 %collective-permute-done.5.refs_2_ = bf16[112,896]{1,0:T(8,128)(2,1)S(1)} collective-permute-done((bf16[112,896]{1,0:T(8,128)(2,1)S(1)}, bf16[112,896]{1,0:T(8,128)(2,1)S(1)}, u32[]{:S(2)}, u32[]{:S(2)}) %collective-permute-start.5) | collective-permute-done | bytes 200736 | tf_op jit(solution)/shard_map/ppermute | solution.py:477
  197.1 11.4 %collective-permute-done.6.refs_3_ = bf16[112,896]{1,0:T(8,128)(2,1)S(1)} collective-permute-done((bf16[112,896]{1,0:T(8,128)(2,1)S(1)}, bf16[112,896]{1,0:T(8,128)(2,1)S(1)}, u32[]{:S(2)}, u32[]{:S(2)}) %collective-permute-start.6) | collective-permute-done | bytes 200736 | tf_op jit(solution)/shard_map/ppermute | solution.py:477
  208.4 1.0 shard_map.53.refs_4_
  209.4 7.8 %collective-permute-done.2.refs_2_ = bf16[112,896]{1,0:T(8,128)(2,1)S(1)} collective-permute-done((bf16[112,896]{1,0:T(8,128)(2,1)S(1)}, bf16[112,896]{1,0:T(8,128)(2,1)S(1)}, u32[]{:S(2)}, u32[]{:S(2)}) %collective-permute-start.2) | collective-permute-done | bytes 200736 | tf_op jit(solution)/shard_map/ppermute | solution.py:477
  217.2 4.3 %collective-permute-done.3.refs_3_ = bf16[112,896]{1,0:T(8,128)(2,1)S(1)} collective-permute-done((bf16[112,896]{1,0:T(8,128)(2,1)S(1)}, bf16[112,896]{1,0:T(8,128)(2,1)S(1)}, u32[]{:S(2)}, u32[]{:S(2)}) %collective-permute-start.3) | collective-permute-done | bytes 200736 | tf_op jit(solution)/shard_map/ppermute | solution.py:477
  221.5 1.0 shard_map.54
  (28 shorter events, 0.2 us)
Async XLA Ops:
  4.6 12.8 %copy-start.4 = (s32[7,3]{0,1:T(4,128)S(1)}, s32[7,3]{0,1:T(4,128)}, u32[]{:S(2)}) copy-start(s32[7,3]{0,1:T(4,128)} %param.7) | copy-start | bytes 256
  4.6 13.0 %copy-start.3 = (f32[6,256]{1,0:T(8,128)S(1)}, f32[6,256]{1,0:T(8,128)}, u32[]{:S(2)}) copy-start(f32[6,256]{1,0:T(8,128)} %param.6) | copy-start | bytes 18436
  4.6 71.1 %all-to-all-start = ((bf16[64,19,8,128]{3,2,1,0:T(8,128)(2,1)}), bf16[64,19,8,128]{3,2,1,0:T(8,128)(2,1)S(1)}, u32[]{:S(2)}, u32[]{:S(2)}) async-start(bf16[64,19,8,128]{3,2,1,0:T(8,128)(2,1)} %shard_map.46), calls=%async_computation | async-start | bytes 4980736 | tf_op jit(solution)/shard_map/all_to_all | solution.py:443
  47.9 6.3 %copy-start.2 = (bf16[3,448,2,512]{3,1,0,2:T(8,128)(2,1)S(1)}, bf16[3,448,2,512]{3,1,0,2:T(8,128)(2,1)}, u32[]{:S(2)}) copy-start(bf16[3,448,2,512]{3,1,0,2:T(8,128)(2,1)} %reshape.773) | copy-start | bytes 8257540
  54.1 2.5 %copy-start.1 = (f32[6,256,896]{2,1,0:T(8,128)}, f32[6,256,896]{2,1,0:T(8,128)S(1)}, u32[]{:S(2)}) copy-start(f32[6,256,896]{2,1,0:T(8,128)S(1)} %shard_map.47.w_hbm) | copy-start | bytes 16515076
  85.0 72.0 %all-to-all-start.1 = ((bf16[256,19,2,128]{3,2,1,0:T(2,128)(2,1)}), bf16[256,19,2,128]{3,2,1,0:T(2,128)(2,1)S(1)}, u32[]{:S(2)}, u32[]{:S(2)}) async-start(bf16[256,19,2,128]{3,2,1,0:T(2,128)(2,1)} %shard_map.48), calls=%async_computation.1 | async-start | bytes 4980736 | tf_op jit(solution)/shard_map/all_to_all | solution.py:468
  161.5 7.5 %collective-permute-start = (bf16[112,896]{1,0:T(8,128)(2,1)S(1)}, bf16[112,896]{1,0:T(8,128)(2,1)S(1)}, u32[]{:S(2)}, u32[]{:S(2)}) collective-permute-start(bf16[112,896]{1,0:T(8,128)(2,1)S(1)} %get-tuple-element.24), channel_id=1, source_target_pairs={{0,1},{1,0},{2,3},{3,2},{4,5},{5,4},{6,7},{7,6},{8,9},{9,8},{10,11... | collective-permute-start | bytes 602120 | tf_op jit(solution)/shard_map/ppermute | solution.py:477
  163.3 19.9 %collective-permute-start.7 = (bf16[112,896]{1,0:T(8,128)(2,1)S(1)}, bf16[112,896]{1,0:T(8,128)(2,1)S(1)}, u32[]{:S(2)}, u32[]{:S(2)}) collective-permute-start(bf16[112,896]{1,0:T(8,128)(2,1)S(1)} %get-tuple-element.37), channel_id=1, source_target_pairs={{0,2},{1,3},{2,0},{3,1},{4,6},{5,7},{6,4},{7,5},{8,10},{9,11},{10,... | collective-permute-start | bytes 602120 | tf_op jit(solution)/shard_map/ppermute | solution.py:477
  163.9 19.4 %collective-permute-start.8 = (bf16[112,896]{1,0:T(8,128)(2,1)S(1)}, bf16[112,896]{1,0:T(8,128)(2,1)S(1)}, u32[]{:S(2)}, u32[]{:S(2)}) collective-permute-start(bf16[112,896]{1,0:T(8,128)(2,1)S(1)} %get-tuple-element.38), channel_id=1, source_target_pairs={{0,3},{1,2},{2,1},{3,0},{4,7},{5,6},{6,5},{7,4},{8,11},{9,10},{10,... | collective-permute-start | bytes 602120 | tf_op jit(solution)/shard_map/ppermute | solution.py:477
  172.9 16.4 %copy-start = (bf16[3,4,112,896]{3,2,1,0:T(8,128)(2,1)S(1)}, bf16[3,4,112,896]{3,2,1,0:T(8,128)(2,1)}, u32[]{:S(2)}) copy-start(bf16[3,4,112,896]{3,2,1,0:T(8,128)(2,1)} %v_ref.5) | copy-start | bytes 7225348
  172.9 10.9 %collective-permute-start.4 = (bf16[112,896]{1,0:T(8,128)(2,1)S(1)}, bf16[112,896]{1,0:T(8,128)(2,1)S(1)}, u32[]{:S(2)}, u32[]{:S(2)}) collective-permute-start(bf16[112,896]{1,0:T(8,128)(2,1)S(1)} %get-tuple-element.32), channel_id=1, source_target_pairs={{0,1},{1,0},{2,3},{3,2},{4,5},{5,4},{6,7},{7,6},{8,9},{9,8},{10,11... | collective-permute-start | bytes 602120 | tf_op jit(solution)/shard_map/ppermute | solution.py:477
  177.1 20.0 %collective-permute-start.5 = (bf16[112,896]{1,0:T(8,128)(2,1)S(1)}, bf16[112,896]{1,0:T(8,128)(2,1)S(1)}, u32[]{:S(2)}, u32[]{:S(2)}) collective-permute-start(bf16[112,896]{1,0:T(8,128)(2,1)S(1)} %get-tuple-element.33), channel_id=1, source_target_pairs={{0,2},{1,3},{2,0},{3,1},{4,6},{5,7},{6,4},{7,5},{8,10},{9,11},{10,... | collective-permute-start | bytes 602120 | tf_op jit(solution)/shard_map/ppermute | solution.py:477
  177.7 30.7 %collective-permute-start.6 = (bf16[112,896]{1,0:T(8,128)(2,1)S(1)}, bf16[112,896]{1,0:T(8,128)(2,1)S(1)}, u32[]{:S(2)}, u32[]{:S(2)}) collective-permute-start(bf16[112,896]{1,0:T(8,128)(2,1)S(1)} %get-tuple-element.34), channel_id=1, source_target_pairs={{0,3},{1,2},{2,1},{3,0},{4,7},{5,6},{6,5},{7,4},{8,11},{9,10},{10,... | collective-permute-start | bytes 602120 | tf_op jit(solution)/shard_map/ppermute | solution.py:477
  183.2 26.2 %collective-permute-start.1 = (bf16[112,896]{1,0:T(8,128)(2,1)S(1)}, bf16[112,896]{1,0:T(8,128)(2,1)S(1)}, u32[]{:S(2)}, u32[]{:S(2)}) collective-permute-start(bf16[112,896]{1,0:T(8,128)(2,1)S(1)} %get-tuple-element.27), channel_id=1, source_target_pairs={{0,1},{1,0},{2,3},{3,2},{4,5},{5,4},{6,7},{7,6},{8,9},{9,8},{10,11... | collective-permute-start | bytes 602120 | tf_op jit(solution)/shard_map/ppermute | solution.py:477
  183.2 34.0 %collective-permute-start.2 = (bf16[112,896]{1,0:T(8,128)(2,1)S(1)}, bf16[112,896]{1,0:T(8,128)(2,1)S(1)}, u32[]{:S(2)}, u32[]{:S(2)}) collective-permute-start(bf16[112,896]{1,0:T(8,128)(2,1)S(1)} %get-tuple-element.28), channel_id=1, source_target_pairs={{0,2},{1,3},{2,0},{3,1},{4,6},{5,7},{6,4},{7,5},{8,10},{9,11},{10,... | collective-permute-start | bytes 602120 | tf_op jit(solution)/shard_map/ppermute | solution.py:477
  183.8 37.7 %collective-permute-start.3 = (bf16[112,896]{1,0:T(8,128)(2,1)S(1)}, bf16[112,896]{1,0:T(8,128)(2,1)S(1)}, u32[]{:S(2)}, u32[]{:S(2)}) collective-permute-start(bf16[112,896]{1,0:T(8,128)(2,1)S(1)} %get-tuple-element.29), channel_id=1, source_target_pairs={{0,3},{1,2},{2,1},{3,0},{4,7},{5,6},{6,5},{7,4},{8,11},{9,10},{10,... | collective-permute-start | bytes 602120 | tf_op jit(solution)/shard_map/ppermute | solution.py:477

commit v5 on v4

--- a/solution.py
+++ b/solution.py
@@ -155,16 +155,17 @@
     order = width // 2
     narrow = order // groups
     share = groups // PARTS
-    arriving = [
-        pltpu.make_async_copy(v_hbm.at[t], v_ref.at[t], in_sems.at[t]) for t in range(channels)
-    ]
-    for copy in arriving:
+    arriving = {
+        (t, z): pltpu.make_async_copy(v_hbm.at[t, z], v_ref.at[t, z], in_sems.at[t, z])
+        for t in range(channels)
+        for z in range(mesh_z)
+    }
+    for copy in arriving.values():
         copy.start()
 
     for t in range(channels):
-        arriving[t].wait()
-
         for z in range(mesh_z):
+            arriving[t, z].wait()
             block = v_ref[t, z].astype(jnp.float32)
             zeros = jnp.zeros((LANES - row_count, width), jnp.float32)
             turned = jnp.concatenate([block, zeros], axis=0).T
@@ -206,7 +207,7 @@
             pltpu.VMEM(vertex.shape, jnp.bfloat16),
             pltpu.VMEM((channels * narrow, groups * 2 * mesh_z, LANES), jnp.float32),
             pltpu.VMEM(shape, jnp.bfloat16),
-            pltpu.SemaphoreType.DMA((channels,)),
+            pltpu.SemaphoreType.DMA((channels, mesh_z)),
             pltpu.SemaphoreType.DMA((PARTS,)),
         ],
         compiler_params=pltpu.CompilerParams(vmem_limit_bytes=32 * 1024 * 1024),
@@ -231,7 +232,7 @@
             step([2 * i, 2 * i + 1])
             return carry
 
-        lax.fori_loop(0, tiles // 2, pair, 0, unroll=3)
+        lax.fori_loop(0, tiles // 2, pair, 0, unroll=True)
         if tiles % 2:
             step([tiles - 1])
 

time: 223 us -> 225 us (level)
  no operation moved by 1% of the time
where the time goes in v5:
time: 225 us; the launch traced here: 224 us
  waiting for transfers between devices  109 us (48%)
  starting transfers between devices  42.3 us (19%)
  Pallas kernels  36.5 us (16%)
  local copies, waits for them, and re-layouts  26.9 us (12%)
  other arithmetic  8.52 us (4%)
    all_to_all x1, waiting for transfers between devices, per_device(): lax.all_to_all(united, ('pb', 'col'), split_axis=0, concat_axis=0, tiled=...  62.3 us
    ppermute x9, waiting for transfers between devices, per_device(): lax.ppermute(pieces[k], 'col', [(i, i ^ k) for i in range(cols)])  30.3 us
    ppermute x9, starting transfers between devices, per_device(): lax.ppermute(pieces[k], 'col', [(i, i ^ k) for i in range(cols)])  19.8 us
    all_to_all x1, waiting for transfers between devices, per_device(): lax.all_to_all(sent, 'pb', split_axis=0, concat_axis=0, tiled=True)  16.1 us
    all_to_all x1, starting transfers between devices, per_device(): lax.all_to_all(sent, 'pb', split_axis=0, concat_axis=0, tiled=True)  12.7 us
    pallas_call x3, Pallas kernels, products(): pl.pallas_call(functools.partial(products_kernel, t), in_specs=[pl.BlockS...  11.8 us
    reshape x2, local copies, waits for them, and re-layouts, per_device(): loops = loop_blocks.reshape(3, order, 2, cols, row_count)  11.2 us
    pallas_call x1, Pallas kernels, transform(): pl.pallas_call(functools.partial(transform_kernel, length), in_specs=[who...  10.4 us
  transfers between devices with their start and end apart: 11, of which 6 were waited for; matrix products, arithmetic and copies ran while one was open for 15% of the time, Pallas kernels for 7%

profile of v5, /device:TPU:1, one launch (start us, length us, event | category | flops | bytes accessed | tf_op | source)
XLA Modules:
  0.0 224.5 jit_solution(16316863347341956799)
XLA Ops:
  0.0 5.2 %shard_map.46 = bf16[64,19,8,128]{3,2,1,0:T(8,128)(2,1)} custom-call(bf16[3,4,112,896]{3,2,1,0:T(8,128)(2,1)} %v_ref.5), custom_call_target="tpu_custom_call" | custom-call | tf_op jit(solution)/shard_map/pallas_call | solution.py:201
  5.2 0.0 copy-start.4
  5.2 0.0 copy-start.3
  5.3 12.7 %all-to-all-start = ((bf16[64,19,8,128]{3,2,1,0:T(8,128)(2,1)}), bf16[64,19,8,128]{3,2,1,0:T(8,128)(2,1)S(1)}, u32[]{:S(2)}, u32[]{:S(2)}) async-start(bf16[64,19,8,128]{3,2,1,0:T(8,128)(2,1)} %shard_map.46), calls=%async_computation | async-start | bytes 4980736 | tf_op jit(solution)/shard_map/all_to_all | solution.py:444
  18.0 0.1 broadcast_reduce_fusion.2
  18.2 0.1 broadcast_reduce_fusion
  18.4 0.4 fusion.1
  18.8 0.6 reshape.776
  19.4 2.1 fusion.36
  21.6 0.1 maximum_bitcast_fusion.2
  21.7 0.5 copy.35
  22.2 0.1 copy.43
  22.3 1.3 maximum_bitcast_fusion
  23.6 0.1 fusion.5
  23.7 0.5 copy.34
  24.2 0.9 copy.42
  25.1 1.3 copy.39.forward_ref
  26.3 8.5 %reshape.772 = bf16[3,448,2,4,112]{4,3,2,1,0:T(4,128)(2,1)} reshape(bf16[3,1,448,896]{3,2,1,0:T(8,128)(2,1)} %param.5) | data formatting | bytes 4816896 | tf_op jit(solution)/shard_map/reshape | solution.py:456
  34.9 2.7 %copy.33 = bf16[3,448,2,4,112]{4,3,1,0,2:T(4,128)(2,1)S(1)} copy(bf16[3,448,2,4,112]{4,3,2,1,0:T(4,128)(2,1)} %reshape.772) | data formatting | bytes 4816896 | tf_op jit(solution)/shard_map/reshape | solution.py:456
  37.6 3.0 %pad.4 = bf16[3,448,2,4,128]{4,3,1,0,2:T(4,128)(2,1)} pad(bf16[3,448,2,4,112]{4,3,1,0,2:T(4,128)(2,1)S(1)} %copy.33, bf16[]{:T(256)} %constant.178.clone.1), padding=0_0x0_0x0_0x0_0x0_16 | pad | bytes 5160962 | tf_op jit(solution)/shard_map/jit(_pad)/pad | solution.py:457
  40.6 5.6 %reshape.773 = bf16[3,448,2,512]{3,1,0,2:T(8,128)(2,1)} reshape(bf16[3,448,2,4,128]{4,3,1,0,2:T(4,128)(2,1)} %pad.4) | data formatting | bytes 5505024 | tf_op jit(solution)/shard_map/reshape | solution.py:457
  46.2 0.1 iota_compare_fusion.3
  46.3 0.1 select_reduce_fusion
  46.4 0.1 fusion.48
  46.5 0.8 reduce-precision_convert_fusion.3
  47.4 0.3 fusion.picks_ref
  47.7 0.5 fusion.14
  48.2 0.1 reduce-precision_convert_fusion.1
  48.3 0.1 reduce-precision_convert_fusion
  48.5 0.1 pad_maximum_fusion.wide_ref
  48.6 6.2 %shard_map.47.w_hbm = f32[6,256,896]{2,1,0:T(8,128)S(1)} custom-call(bf16[7,256,256]{2,1,0:T(8,128)(2,1)S(1)} %fusion.picks_ref, bf16[256,2304]{1,0:T(8,128)(2,1)S(1)} %pad_maximum_fusion.wide_ref), custom_call_target="tpu_custom_call" | custom-call | tf_op jit(solution)/shard_map/pallas_call | solution.py:83
  54.8 0.1 fusion.73
  54.9 0.2 slice_bitcast_fusion
  55.1 2.2 copy-done.1
  57.3 3.0 %maximum_maximum_fusion.loop_hbm = bf16[3,896,1024]{2,1,0:T(8,128)(2,1)} fusion(bf16[3,448,512]{2,1,0:T(8,128)(2,1)S(1)} %get-tuple-element.42, bf16[3,448,512]{2,1,0:T(8,128)(2,1)S(1)} %fusion.73, bf16[3,448,512]{2,1,0:T(8,128)(2,1)S(1)} %get-tuple-element.41), kind=kLoop, calls=%fused_computation | loop fusion | flops 22020096 | bytes 9633792 | tf_op jit(solution)/shard_map/concatenate | solution.py:459
  60.2 16.1 %all-to-all-done.x_ref = bf16[64,19,8,128]{3,2,1,0:T(8,128)(2,1)S(1)} async-done(((bf16[64,19,8,128]{3,2,1,0:T(8,128)(2,1)}), bf16[64,19,8,128]{3,2,1,0:T(8,128)(2,1)S(1)}, u32[]{:S(2)}, u32[]{:S(2)}) %all-to-all-start) | async-done | bytes 2490400 | tf_op jit(solution)/shard_map/all_to_all | solution.py:444
  76.4 10.4 %shard_map.48 = bf16[256,19,2,128]{3,2,1,0:T(2,128)(2,1)} custom-call(bf16[64,19,8,128]{3,2,1,0:T(8,128)(2,1)S(1)} %all-to-all-done.x_ref, bf16[512,512]{1,0:T(8,128)(2,1)S(1)} %copy.39.forward_ref, bf16[512,512]{1,0:T(8,128)(2,1)S(1)} %bitcast.56, f32[6,256,896]{2,1,0:T(8,128)} %copy-done.1), custom_call_target="tpu_custom_call" | custom-call | tf_op jit(solution)/shard_map/pallas_call | solution.py:297
  86.8 9.7 %all-to-all-start.1 = ((bf16[256,19,2,128]{3,2,1,0:T(2,128)(2,1)}), bf16[256,19,2,128]{3,2,1,0:T(2,128)(2,1)S(1)}, u32[]{:S(2)}, u32[]{:S(2)}) async-start(bf16[256,19,2,128]{3,2,1,0:T(2,128)(2,1)} %shard_map.48), calls=%async_computation.1 | async-start | bytes 4980736 | tf_op jit(solution)/shard_map/all_to_all | solution.py:469
  96.5 62.3 %all-to-all-done.1 = bf16[256,19,2,128]{3,2,1,0:T(2,128)(2,1)S(1)} async-done(((bf16[256,19,2,128]{3,2,1,0:T(2,128)(2,1)}), bf16[256,19,2,128]{3,2,1,0:T(2,128)(2,1)S(1)}, u32[]{:S(2)}, u32[]{:S(2)}) %all-to-all-start.1) | async-done | bytes 2490400 | tf_op jit(solution)/shard_map/all_to_all | solution.py:469
  158.9 0.6 copy.45
  159.4 3.9 %shard_map.49 = (bf16[112,896]{1,0:T(8,128)(2,1)S(1)}, bf16[112,896]{1,0:T(8,128)(2,1)S(1)}, bf16[112,896]{1,0:T(8,128)(2,1)S(1)}, bf16[112,896]{1,0:T(8,128)(2,1)S(1)}) custom-call(s32[1]{0:T(128)} %bitcast.mine_ref, bf16[19,2,256,128]{3,2,1,0:T(8,128)(2,1)S(1)} %bitcast.53, bf16[3,896,1024]{2,1,0:T(8,128)(2,1)} %maximum_maximum_fusion.loop_hbm), custom_call_target="tpu_custom_call" | custom-call | tf_op jit(solution)/shard_map/pallas_call | solution.py:374
  163.3 1.8 collective-permute-start
  165.1 0.5 collective-permute-start.7
  165.7 5.1 %collective-permute-start.8 = (bf16[112,896]{1,0:T(8,128)(2,1)S(1)}, bf16[112,896]{1,0:T(8,128)(2,1)S(1)}, u32[]{:S(2)}, u32[]{:S(2)}) collective-permute-start(bf16[112,896]{1,0:T(8,128)(2,1)S(1)} %get-tuple-element.38), channel_id=1, source_target_pairs={{0,3},{1,2},{2,1},{3,0},{4,7},{5,6},{6,5},{7,4},{8,11},{9,10},{10,... | collective-permute-start | bytes 602120 | tf_op jit(solution)/shard_map/ppermute | solution.py:478
  170.8 0.0 collective-permute-done.refs_1_
  170.8 3.9 %shard_map.51 = (bf16[112,896]{1,0:T(8,128)(2,1)S(1)}, bf16[112,896]{1,0:T(8,128)(2,1)S(1)}, bf16[112,896]{1,0:T(8,128)(2,1)S(1)}, bf16[112,896]{1,0:T(8,128)(2,1)S(1)}) custom-call(s32[1]{0:T(128)} %bitcast.mine_ref, bf16[19,2,256,128]{3,2,1,0:T(8,128)(2,1)S(1)} %bitcast.54, bf16[3,896,1024]{2,1,0:T(8,128)(2,1)} %maximum_maximum_fusion.loop_hbm), custom_call_target="tpu_custom_call" | custom-call | tf_op jit(solution)/shard_map/pallas_call | solution.py:374
  174.7 0.0 copy-start
  174.7 0.2 collective-permute-start.4
  174.9 4.0 %shard_map.50 = (bf16[112,896]{1,0:T(8,128)(2,1)S(1)}, bf16[112,896]{1,0:T(8,128)(2,1)S(1)}, bf16[112,896]{1,0:T(8,128)(2,1)S(1)}, bf16[112,896]{1,0:T(8,128)(2,1)S(1)}) custom-call(s32[1]{0:T(128)} %bitcast.mine_ref, bf16[19,2,256,128]{3,2,1,0:T(8,128)(2,1)S(1)} %bitcast.55, bf16[3,896,1024]{2,1,0:T(8,128)(2,1)} %maximum_maximum_fusion.loop_hbm), custom_call_target="tpu_custom_call" | custom-call | tf_op jit(solution)/shard_map/pallas_call | solution.py:374
  178.9 0.6 collective-permute-start.5
  179.5 5.5 %collective-permute-start.6 = (bf16[112,896]{1,0:T(8,128)(2,1)S(1)}, bf16[112,896]{1,0:T(8,128)(2,1)S(1)}, u32[]{:S(2)}, u32[]{:S(2)}) collective-permute-start(bf16[112,896]{1,0:T(8,128)(2,1)S(1)} %get-tuple-element.34), channel_id=1, source_target_pairs={{0,3},{1,2},{2,1},{3,0},{4,7},{5,6},{6,5},{7,4},{8,11},{9,10},{10,... | collective-permute-start | bytes 602120 | tf_op jit(solution)/shard_map/ppermute | solution.py:478
  185.0 0.0 collective-permute-done.7.refs_2_
  185.0 0.0 collective-permute-start.1
  185.0 0.0 collective-permute-done.8.refs_3_
  185.0 0.6 collective-permute-start.2
  185.6 0.0 collective-permute-done.4.refs_1_
  185.6 5.5 %collective-permute-start.3 = (bf16[112,896]{1,0:T(8,128)(2,1)S(1)}, bf16[112,896]{1,0:T(8,128)(2,1)S(1)}, u32[]{:S(2)}, u32[]{:S(2)}) collective-permute-start(bf16[112,896]{1,0:T(8,128)(2,1)S(1)} %get-tuple-element.29), channel_id=1, source_target_pairs={{0,3},{1,2},{2,1},{3,0},{4,7},{5,6},{6,5},{7,4},{8,11},{9,10},{10,... | collective-permute-start | bytes 602120 | tf_op jit(solution)/shard_map/ppermute | solution.py:478
  191.1 1.0 shard_map.52.refs_4_
  192.0 6.8 %collective-permute-done.5.refs_2_ = bf16[112,896]{1,0:T(8,128)(2,1)S(1)} collective-permute-done((bf16[112,896]{1,0:T(8,128)(2,1)S(1)}, bf16[112,896]{1,0:T(8,128)(2,1)S(1)}, u32[]{:S(2)}, u32[]{:S(2)}) %collective-permute-start.5) | collective-permute-done | bytes 200736 | tf_op jit(solution)/shard_map/ppermute | solution.py:478
  198.8 11.4 %collective-permute-done.6.refs_3_ = bf16[112,896]{1,0:T(8,128)(2,1)S(1)} collective-permute-done((bf16[112,896]{1,0:T(8,128)(2,1)S(1)}, bf16[112,896]{1,0:T(8,128)(2,1)S(1)}, u32[]{:S(2)}, u32[]{:S(2)}) %collective-permute-start.6) | collective-permute-done | bytes 200736 | tf_op jit(solution)/shard_map/ppermute | solution.py:478
  210.2 1.0 shard_map.53.refs_4_
  211.2 7.8 %collective-permute-done.2.refs_2_ = bf16[112,896]{1,0:T(8,128)(2,1)S(1)} collective-permute-done((bf16[112,896]{1,0:T(8,128)(2,1)S(1)}, bf16[112,896]{1,0:T(8,128)(2,1)S(1)}, u32[]{:S(2)}, u32[]{:S(2)}) %collective-permute-start.2) | collective-permute-done | bytes 200736 | tf_op jit(solution)/shard_map/ppermute | solution.py:478
  219.0 4.3 %collective-permute-done.3.refs_3_ = bf16[112,896]{1,0:T(8,128)(2,1)S(1)} collective-permute-done((bf16[112,896]{1,0:T(8,128)(2,1)S(1)}, bf16[112,896]{1,0:T(8,128)(2,1)S(1)}, u32[]{:S(2)}, u32[]{:S(2)}) %collective-permute-start.3) | collective-permute-done | bytes 200736 | tf_op jit(solution)/shard_map/ppermute | solution.py:478
  223.3 1.0 shard_map.54
  (28 shorter events, 0.2 us)
Async XLA Ops:
  5.2 12.8 %copy-start.4 = (s32[7,3]{0,1:T(4,128)S(1)}, s32[7,3]{0,1:T(4,128)}, u32[]{:S(2)}) copy-start(s32[7,3]{0,1:T(4,128)} %param.7) | copy-start | bytes 256
  5.2 13.0 %copy-start.3 = (f32[6,256]{1,0:T(8,128)S(1)}, f32[6,256]{1,0:T(8,128)}, u32[]{:S(2)}) copy-start(f32[6,256]{1,0:T(8,128)} %param.6) | copy-start | bytes 18436
  5.3 71.1 %all-to-all-start = ((bf16[64,19,8,128]{3,2,1,0:T(8,128)(2,1)}), bf16[64,19,8,128]{3,2,1,0:T(8,128)(2,1)S(1)}, u32[]{:S(2)}, u32[]{:S(2)}) async-start(bf16[64,19,8,128]{3,2,1,0:T(8,128)(2,1)} %shard_map.46), calls=%async_computation | async-start | bytes 4980736 | tf_op jit(solution)/shard_map/all_to_all | solution.py:444
  48.5 6.3 %copy-start.2 = (bf16[3,448,2,512]{3,1,0,2:T(8,128)(2,1)S(1)}, bf16[3,448,2,512]{3,1,0,2:T(8,128)(2,1)}, u32[]{:S(2)}) copy-start(bf16[3,448,2,512]{3,1,0,2:T(8,128)(2,1)} %reshape.773) | copy-start | bytes 8257540
  54.8 2.5 %copy-start.1 = (f32[6,256,896]{2,1,0:T(8,128)}, f32[6,256,896]{2,1,0:T(8,128)S(1)}, u32[]{:S(2)}) copy-start(f32[6,256,896]{2,1,0:T(8,128)S(1)} %shard_map.47.w_hbm) | copy-start | bytes 16515076
  86.8 72.0 %all-to-all-start.1 = ((bf16[256,19,2,128]{3,2,1,0:T(2,128)(2,1)}), bf16[256,19,2,128]{3,2,1,0:T(2,128)(2,1)S(1)}, u32[]{:S(2)}, u32[]{:S(2)}) async-start(bf16[256,19,2,128]{3,2,1,0:T(2,128)(2,1)} %shard_map.48), calls=%async_computation.1 | async-start | bytes 4980736 | tf_op jit(solution)/shard_map/all_to_all | solution.py:469
  163.3 7.4 %collective-permute-start = (bf16[112,896]{1,0:T(8,128)(2,1)S(1)}, bf16[112,896]{1,0:T(8,128)(2,1)S(1)}, u32[]{:S(2)}, u32[]{:S(2)}) collective-permute-start(bf16[112,896]{1,0:T(8,128)(2,1)S(1)} %get-tuple-element.24), channel_id=1, source_target_pairs={{0,1},{1,0},{2,3},{3,2},{4,5},{5,4},{6,7},{7,6},{8,9},{9,8},{10,11... | collective-permute-start | bytes 602120 | tf_op jit(solution)/shard_map/ppermute | solution.py:478
  165.1 19.9 %collective-permute-start.7 = (bf16[112,896]{1,0:T(8,128)(2,1)S(1)}, bf16[112,896]{1,0:T(8,128)(2,1)S(1)}, u32[]{:S(2)}, u32[]{:S(2)}) collective-permute-start(bf16[112,896]{1,0:T(8,128)(2,1)S(1)} %get-tuple-element.37), channel_id=1, source_target_pairs={{0,2},{1,3},{2,0},{3,1},{4,6},{5,7},{6,4},{7,5},{8,10},{9,11},{10,... | collective-permute-start | bytes 602120 | tf_op jit(solution)/shard_map/ppermute | solution.py:478
  165.7 19.4 %collective-permute-start.8 = (bf16[112,896]{1,0:T(8,128)(2,1)S(1)}, bf16[112,896]{1,0:T(8,128)(2,1)S(1)}, u32[]{:S(2)}, u32[]{:S(2)}) collective-permute-start(bf16[112,896]{1,0:T(8,128)(2,1)S(1)} %get-tuple-element.38), channel_id=1, source_target_pairs={{0,3},{1,2},{2,1},{3,0},{4,7},{5,6},{6,5},{7,4},{8,11},{9,10},{10,... | collective-permute-start | bytes 602120 | tf_op jit(solution)/shard_map/ppermute | solution.py:478
  174.7 16.4 %copy-start = (bf16[3,4,112,896]{3,2,1,0:T(8,128)(2,1)S(1)}, bf16[3,4,112,896]{3,2,1,0:T(8,128)(2,1)}, u32[]{:S(2)}) copy-start(bf16[3,4,112,896]{3,2,1,0:T(8,128)(2,1)} %v_ref.5) | copy-start | bytes 7225348
  174.7 10.9 %collective-permute-start.4 = (bf16[112,896]{1,0:T(8,128)(2,1)S(1)}, bf16[112,896]{1,0:T(8,128)(2,1)S(1)}, u32[]{:S(2)}, u32[]{:S(2)}) collective-permute-start(bf16[112,896]{1,0:T(8,128)(2,1)S(1)} %get-tuple-element.32), channel_id=1, source_target_pairs={{0,1},{1,0},{2,3},{3,2},{4,5},{5,4},{6,7},{7,6},{8,9},{9,8},{10,11... | collective-permute-start | bytes 602120 | tf_op jit(solution)/shard_map/ppermute | solution.py:478
  178.9 19.9 %collective-permute-start.5 = (bf16[112,896]{1,0:T(8,128)(2,1)S(1)}, bf16[112,896]{1,0:T(8,128)(2,1)S(1)}, u32[]{:S(2)}, u32[]{:S(2)}) collective-permute-start(bf16[112,896]{1,0:T(8,128)(2,1)S(1)} %get-tuple-element.33), channel_id=1, source_target_pairs={{0,2},{1,3},{2,0},{3,1},{4,6},{5,7},{6,4},{7,5},{8,10},{9,11},{10,... | collective-permute-start | bytes 602120 | tf_op jit(solution)/shard_map/ppermute | solution.py:478
  179.5 30.7 %collective-permute-start.6 = (bf16[112,896]{1,0:T(8,128)(2,1)S(1)}, bf16[112,896]{1,0:T(8,128)(2,1)S(1)}, u32[]{:S(2)}, u32[]{:S(2)}) collective-permute-start(bf16[112,896]{1,0:T(8,128)(2,1)S(1)} %get-tuple-element.34), channel_id=1, source_target_pairs={{0,3},{1,2},{2,1},{3,0},{4,7},{5,6},{6,5},{7,4},{8,11},{9,10},{10,... | collective-permute-start | bytes 602120 | tf_op jit(solution)/shard_map/ppermute | solution.py:478
  185.0 26.2 %collective-permute-start.1 = (bf16[112,896]{1,0:T(8,128)(2,1)S(1)}, bf16[112,896]{1,0:T(8,128)(2,1)S(1)}, u32[]{:S(2)}, u32[]{:S(2)}) collective-permute-start(bf16[112,896]{1,0:T(8,128)(2,1)S(1)} %get-tuple-element.27), channel_id=1, source_target_pairs={{0,1},{1,0},{2,3},{3,2},{4,5},{5,4},{6,7},{7,6},{8,9},{9,8},{10,11... | collective-permute-start | bytes 602120 | tf_op jit(solution)/shard_map/ppermute | solution.py:478
  185.0 34.0 %collective-permute-start.2 = (bf16[112,896]{1,0:T(8,128)(2,1)S(1)}, bf16[112,896]{1,0:T(8,128)(2,1)S(1)}, u32[]{:S(2)}, u32[]{:S(2)}) collective-permute-start(bf16[112,896]{1,0:T(8,128)(2,1)S(1)} %get-tuple-element.28), channel_id=1, source_target_pairs={{0,2},{1,3},{2,0},{3,1},{4,6},{5,7},{6,4},{7,5},{8,10},{9,11},{10,... | collective-permute-start | bytes 602120 | tf_op jit(solution)/shard_map/ppermute | solution.py:478
  185.6 37.7 %collective-permute-start.3 = (bf16[112,896]{1,0:T(8,128)(2,1)S(1)}, bf16[112,896]{1,0:T(8,128)(2,1)S(1)}, u32[]{:S(2)}, u32[]{:S(2)}) collective-permute-start(bf16[112,896]{1,0:T(8,128)(2,1)S(1)} %get-tuple-element.29), channel_id=1, source_target_pairs={{0,3},{1,2},{2,1},{3,0},{4,7},{5,6},{6,5},{7,4},{8,11},{9,10},{10,... | collective-permute-start | bytes 602120 | tf_op jit(solution)/shard_map/ppermute | solution.py:478
